TPU v7x, 512 devices: a whole 4x4x16 slice. The times are simulated.
512 devices in a mesh: ctx: 64 (over y, z_lo, core), dp: 8 (over z_hi, x).
Axes of the slice: x: 4, y: 4, z: 16 (z_hi: 2, z_lo: 8; z = z_hi * 8 + z_lo), core: 2. Of those that a mesh axis runs over, the one named last changes fastest.
Arguments:
- tokens: bfloat16 [8, 8192, 4096], P('dp', 'ctx'), may hold values from -64 to 64
- stretch_table: int32 [64, 2], replicated, may hold values from 0 to 127, as said below
- query_weight: bfloat16 [4096, 512], P(('ctx', 'dp')), may hold values from -1 to 1
- key_weight: bfloat16 [4096, 128], P(('ctx', 'dp')), may hold values from -1 to 1
- value_weight: bfloat16 [4096, 128], P(('ctx', 'dp')), may hold values from -0.09375 to 0.09375
Outputs:
- attended: bfloat16 [8, 8192, 512], P('dp', 'ctx')
Inputs may be any that keep to these rules, and one draw needn't show every extreme that they name: `stretch_table`: row r names stretches c and 127 - c for some c < 64, in either order; every stretch of the sequence is named once.
All inputs are finite; a program needn't handle non-finite values.
Results may differ from a plain program's by a relative error of at most 0.012.
Values may be sent and summed in bfloat16 or wider, within the bound.
No kernel may reach another device: no remote copies, remote signals or barrier semaphores. Data moves between devices by JAX's collectives and lax.ppermute only.
A program may use at most 64 MiB of HBM per device.

v0:
```python
import math

import jax
import jax.numpy as jnp
from jax import lax
from jax.sharding import PartitionSpec as P

rope_base = 500000.0
masked_fill = -1e30


def side_by_side(arrays, axis, dim, along):
    widths = [a.shape[along] for a in arrays]
    both = jnp.concatenate(arrays, axis=along)
    whole = lax.all_gather(both, axis, axis=dim, tiled=True)
    return tuple(jnp.split(whole, [sum(widths[:k]) for k in range(1, len(widths))], axis=along))


def rotate(vectors, positions):
    head_width = vectors.shape[-1]
    half_width = head_width // 2
    frequency = rope_base ** (-(jnp.arange(half_width, dtype=jnp.float32) * 2.0 / head_width))
    angles = positions.astype(jnp.float32)[:, None] * frequency[None, :]
    cosine = jnp.cos(angles)[:, None, :]
    sine_part = jnp.sin(angles)[:, None, :]
    first_half = vectors[..., :half_width]
    second_half = vectors[..., half_width:]
    return jnp.concatenate(
        [
            first_half * cosine - second_half * sine_part,
            second_half * cosine + first_half * sine_part,
        ],
        axis=-1,
    )


def unchanged(carried):
    return carried


def on_device(tokens, stretch_table, query_weight, key_weight, value_weight):
    token_rows = tokens[0]
    row_count = token_rows.shape[0]
    half_rows = row_count // 2
    head_width = key_weight.shape[1]
    head_count = query_weight.shape[1] // head_width
    score_scale = 1.0 / math.sqrt(head_width)
    offsets = jnp.arange(half_rows, dtype=jnp.int32)
    grouped = side_by_side((query_weight, key_weight, value_weight), "dp", 0, 1)
    pieces = side_by_side((grouped[0], grouped[1], grouped[2]), "ctx", 0, 1)
    query_full, key_full, value_full = tuple(
        (
            jnp.dot(token_rows, weight_piece, preferred_element_type=jnp.float32)
            for weight_piece in pieces
        )
    )
    own_index = lax.axis_index("ctx")
    own_stretches = lax.dynamic_index_in_dim(stretch_table, own_index, 0, keepdims=False)
    query_pos = jnp.concatenate(
        [own_stretches[0] * half_rows + offsets, own_stretches[1] * half_rows + offsets]
    )
    queries = rotate(query_full.reshape(row_count, head_count, head_width), query_pos).astype(
        jnp.bfloat16
    )
    keys_own = rotate(key_full[:, None, :], query_pos)[:, 0, :].astype(jnp.bfloat16)
    values_own = value_full.astype(jnp.bfloat16)
    query_halves = queries.reshape(2, half_rows, head_count, head_width)

    def attend(softmax_state, key_block, value_block, source):
        key_stretches = lax.dynamic_index_in_dim(stretch_table, source, 0, keepdims=False)
        maxima, totals, weighted = softmax_state
        new_max = []
        new_sum = []
        new_acc = []
        for query_half in range(2):
            running = (maxima[query_half], totals[query_half], weighted[query_half])
            query_pos_half = own_stretches[query_half] * half_rows + offsets
            for key_half in range(2):
                key_rows = key_block[key_half * half_rows : (key_half + 1) * half_rows]
                value_rows = value_block[key_half * half_rows : (key_half + 1) * half_rows]
                key_pos = key_stretches[key_half] * half_rows + offsets

                def compute(
                    carried,
                    key_rows=key_rows,
                    value_rows=value_rows,
                    key_pos=key_pos,
                    query_pos_half=query_pos_half,
                    query_half=query_half,
                ):
                    row_max, row_sum, row_acc = carried
                    scores = (
                        jnp.einsum(
                            "qhd,kd->hqk",
                            query_halves[query_half],
                            key_rows,
                            preferred_element_type=jnp.float32,
                        )
                        * score_scale
                    )
                    allowed = key_pos[None, None, :] <= query_pos_half[None, :, None]
                    scores = jnp.where(allowed, scores, masked_fill)
                    next_max = jnp.maximum(row_max, jnp.max(scores, axis=-1))
                    probabilities = jnp.where(
                        allowed, jnp.exp(scores - next_max[:, :, None]), 0.0
                    ).astype(jnp.bfloat16)
                    rescale = jnp.exp(row_max - next_max)
                    row_sum = row_sum * rescale + jnp.sum(
                        probabilities.astype(jnp.float32), axis=-1
                    )
                    row_acc = row_acc * jnp.transpose(rescale)[:, :, None] + jnp.einsum(
                        "hqk,kd->qhd", probabilities, value_rows, preferred_element_type=jnp.float32
                    )
                    return (next_max, row_sum, row_acc)

                running = lax.cond(
                    key_stretches[key_half] <= own_stretches[query_half],
                    compute,
                    unchanged,
                    running,
                )
            new_max.append(running[0])
            new_sum.append(running[1])
            new_acc.append(running[2])
        return (jnp.stack(new_max), jnp.stack(new_sum), jnp.stack(new_acc))

    empty_state = (
        jnp.full((2, head_count, half_rows), masked_fill, jnp.float32),
        jnp.zeros((2, head_count, half_rows), jnp.float32),
        jnp.zeros((2, half_rows, head_count, head_width), jnp.float32),
    )
    pieces = side_by_side((keys_own, values_own), "ctx", 0, 1)
    shard_count = pieces[0].shape[0] // row_count

    def fold_shard(step_index, running_state):
        key_block = lax.dynamic_slice_in_dim(pieces[0], step_index * row_count, row_count, 0)
        value_block = lax.dynamic_slice_in_dim(pieces[1], step_index * row_count, row_count, 0)
        return attend(running_state, key_block, value_block, step_index)

    final_state = lax.fori_loop(0, shard_count, fold_shard, empty_state)
    maxima, totals, weighted = final_state
    attended = weighted / jnp.transpose(totals, (0, 2, 1))[:, :, :, None]
    return attended.reshape(row_count, head_count * head_width).astype(jnp.bfloat16)[None]


def solution(mesh):
    placed = (
        P("dp", "ctx", None),
        P(),
        P(("ctx", "dp"), None),
        P(("ctx", "dp"), None),
        P(("ctx", "dp"), None),
    )
    return jax.shard_map(
        on_device, mesh=mesh, in_specs=placed, out_specs=P("dp", "ctx", None), check_vma=False
    )
```

profile of v0, /device:TPU:19, one launch (start us, length us, event | category | flops | bytes accessed | tf_op | source)
XLA Modules:
  0.0 1476.2 jit_solution(7461732986666156602)
XLA Ops:
  7.4 62.4 %all_gather.9 = bf16[64,768]{1,0:T(8,128)(2,1)} all-gather(bf16[8,768]{1,0:T(8,128)(2,1)S(1)} %pad_maximum_fusion.5), channel_id=1, replica_groups=mesh['ctx'=64,'dp'=8] {'dp'}, dimensions={0}, use_global_device_ids=true | all-gather | bytes 110592 | tf_op jit(solution)/shard_map/all_gather | solution.py:15
  72.6 128.2 %all-gather.3.cloned.1.call-done = bf16[4096,768]{1,0:T(8,128)(2,1)} async-done(((bf16[64,768]{1,0:T(8,128)(2,1)}), bf16[4096,768]{1,0:T(8,128)(2,1)}) %all-gather.3.cloned.1.call-update) | async-done | bytes 6291472 | tf_op jit(solution)/shard_map/all_gather | solution.py:15
  205.4 3.5 fusion.40
  209.7 117.6 %all-gather.5.cloned.1.call-done = bf16[8192,256]{0,1:T(8,128)(2,1)} async-done(((bf16[128,256]{0,1:T(8,128)(2,1)}), bf16[8192,256]{0,1:T(8,128)(2,1)}) %all-gather.5.cloned.1.call-update) | async-done | bytes 4194320 | tf_op jit(solution)/shard_map/all_gather | solution.py:15
  327.3 4.6 fusion.63
  331.9 1136.4 %while.20 = (s32[]{:T(128)}, f32[2,4,64]{2,1,0:T(4,128)S(1)}, f32[2,4,64]{2,1,0:T(4,128)S(1)}, f32[2,64,4,128]{3,1,2,0:T(8,128)S(1)}, s32[64,2]{0,1:T(2,128)S(1)...) while((s32[]{:T(128)}, f32[2,4,64]{2,1,0:T(4,128)S(1)}, ...), condition=%wide.region_17.18_spmd.clone.clone, body=%wide.region_0.17_spmd.clone.clone.sunk | while | flops 34623756 | bytes 3706651 | solution.py:140
  381.8 3.2 conditional.17
  434.9 3.2 conditional.17
  453.2 3.2 conditional.17
  539.7 3.2 conditional.17
  558.1 3.2 conditional.17
  611.2 3.2 conditional.17
  682.8 3.2 conditional.17
  718.2 3.2 conditional.17
  772.0 3.2 conditional.17
  878.3 3.2 conditional.17
  933.9 3.2 conditional.17
  987.7 3.2 conditional.17
  1076.9 3.2 conditional.17
  1095.4 3.2 conditional.17
  1218.7 3.2 conditional.17
  1237.1 3.2 conditional.17
  1307.2 3.2 conditional.17
  1342.6 3.2 conditional.17
  (2259 shorter events, 1034.5 us)
Async XLA Ops:
  6.5 194.3 %copy-start = (bf16[1,128,4096]{2,1,0:T(8,128)(2,1)S(1)}, bf16[1,128,4096]{2,1,0:T(8,128)(2,1)}, u32[]{:S(2)}) copy-start(bf16[1,128,4096]{2,1,0:T(8,128)(2,1)} %param.15) | copy-start | bytes 3145732
  6.5 194.3 %all-gather.3.cloned.1.call-start = ((), (), s32[]{:S(2)}) async-start(), calls=%async_computation | async-start | bytes 6389760 | tf_op jit(solution)/shard_map/all_gather | solution.py:15
  69.8 257.5 %all-gather.5.cloned.1.call-start = ((), (), s32[]{:S(2)}) async-start(), calls=%async_computation.1 | async-start | bytes 4259840 | tf_op jit(solution)/shard_map/all_gather | solution.py:15
  209.7 122.2 %copy-start.1 = (s32[64,2]{0,1:T(2,128)S(1)}, s32[64,2]{0,1:T(2,128)}, u32[]{:S(2)}) copy-start(s32[64,2]{0,1:T(2,128)} %param.16) | copy-start | bytes 1540
Sparse Core Ops, SparseCore 0:
  69.9 130.9 all-gather.2
  205.3 121.9 all-gather.4
where the time goes:
time: 1500 us; the launch traced here: 1480 us
  loops' own time  427 us (28%)
  local copies, waits for them, and re-layouts  336 us (22%)
  other arithmetic  282 us (19%)
  waiting for transfers between devices  246 us (16%)
  matrix products  108 us (7%)
  blocking collectives  62.4 us (4%)
    another operation x1, loops' own time, on_device(): final_state = lax.fori_loop(0, shard_count, fold_shard, empty_state)  423 us
    all_gather x2, waiting for transfers between devices, side_by_side(): whole = lax.all_gather(both, axis, axis=dim, tiled=True)  246 us
    while x384, local copies, waits for them, and re-layouts  111 us
    another operation x257, other arithmetic, attend(): return (jnp.stack(new_max), jnp.stack(new_sum), jnp.stack(new_acc))  91 us
    transpose x129, other arithmetic, compute(): jnp.transpose(rescale)[:, :, None]  82.5 us
    dot_general x129, matrix products, compute(): jnp.einsum('hqk,kd->qhd', probabilities, value_rows, preferred_element_ty...  73.9 us
    all_gather x1, blocking collectives, side_by_side(): whole = lax.all_gather(both, axis, axis=dim, tiled=True)  62.4 us
    slice x64, local copies, waits for them, and re-layouts, attend(): value_rows = value_block[key_half * half_rows:(key_half + 1) * half_rows]  60.3 us
  transfers between devices with their start and end apart: 2, of which 2 were waited for; matrix products, arithmetic and copies ran while one was open for 0% of the time, Pallas kernels for 0%

commit v1 on v0

v1 whole, which is shorter than its diff:
```python
import math

import jax
import jax.numpy as jnp
from jax import lax
from jax.experimental import pallas as pl
from jax.experimental.pallas import tpu as pltpu
from jax.sharding import Mesh, PartitionSpec as P

rope_base = 500000.0
masked_fill = -1e30
HEAD = 128
HEADS = 4
STRETCH = 64
ROWS = 128
KEYS = 2048
CHUNK = 512
score_scale = 1.0 / math.sqrt(HEAD)
exponent_scale = score_scale * math.log2(math.e)

vmem = pl.BlockSpec(memory_space=pltpu.VMEM)
smem = pl.BlockSpec(memory_space=pltpu.SMEM)


def swap(value, axis, size, distance):
    return lax.ppermute(value, axis, [(i, i ^ distance) for i in range(size)])


def spread(value, axis, size):
    copies = jnp.broadcast_to(value[None], (size,) + value.shape)
    return lax.all_to_all(copies, axis, 0, 0)


def angle_tables(positions):
    half = HEAD // 2
    frequency = rope_base ** (-(jnp.arange(half, dtype=jnp.float32) * 2.0 / HEAD))
    angles = positions.astype(jnp.float32)[:, None] * frequency[None, :]
    cosine = jnp.cos(angles)
    sine = jnp.sin(angles)
    return (
        jnp.concatenate([cosine, cosine], axis=1),
        jnp.concatenate([-sine, sine], axis=1),
    )


def key_value_kernel(parts, cosine, sine, out):
    total = parts[0] + parts[1] + parts[2] + parts[3]
    key = total[:, :HEAD]
    turned = key * cosine[...] + pltpu.roll(key, HEAD // 2, 1) * sine[...]
    out[:, :HEAD] = turned.astype(jnp.bfloat16)
    out[:, HEAD:] = total[:, HEAD:].astype(jnp.bfloat16)


def query_kernel(parts, cosine, sine, out):
    for head in range(HEADS):
        span = slice(head * HEAD, (head + 1) * HEAD)
        total = parts[0, :, span] + parts[1, :, span] + parts[2, :, span] + parts[3, :, span]
        turned = total * cosine[...] + pltpu.roll(total, HEAD // 2, 1) * sine[...]
        turned = turned.astype(jnp.bfloat16)
        for slot in range(2):
            row = (slot * HEADS + head) * STRETCH
            out[row : row + STRETCH, :] = turned[slot * STRETCH : (slot + 1) * STRETCH]


def attention_kernel(plan, query, own_near, own_far, other_near, other_far, out, keys, values, scores):
    pieces = (own_near, own_far, other_near, other_far)
    values[:, HEAD:] = jnp.ones((KEYS, HEAD), jnp.bfloat16)
    for index in range(KEYS // STRETCH):
        piece = pieces[index // 8]
        source = (index % 8) * STRETCH
        target = pl.multiple_of(plan[index] * STRETCH, STRETCH)
        keys[pl.ds(target, STRETCH), :] = piece[source : source + STRETCH, :HEAD]
        values[pl.ds(target, STRETCH), :HEAD] = piece[source : source + STRETCH, HEAD:]
    rows = HEADS * STRETCH
    stretch_row = lax.broadcasted_iota(jnp.int32, (rows, CHUNK), 0) % STRETCH
    lane = lax.broadcasted_iota(jnp.int32, (rows, CHUNK), 1)
    small_lane = lax.broadcasted_iota(jnp.int32, (STRETCH, HEAD), 1)
    own_row = plan[40]
    for index in range(8):
        peer = index // 2
        slot = index % 2
        full = plan[32 + index] * STRETCH
        here = (own_row == peer).astype(jnp.int32)
        chunks = (full + here * STRETCH + CHUNK - 1) // CHUNK
        limit = lane - stretch_row * here
        q = query[index * rows : (index + 1) * rows, :]

        def score(chunk, running, q=q, limit=limit, full=full, here=here):
            start = pl.multiple_of(chunk * CHUNK, CHUNK)
            s = lax.dot_general(
                q, keys[pl.ds(start, CHUNK), :], (((1,), (1,)), ((), ())),
                preferred_element_type=jnp.float32,
            )
            s = jnp.where(limit < full + here - start, s, masked_fill)
            scores[chunk] = s
            for part in range(CHUNK // HEAD):
                running = jnp.maximum(running, s[:, part * HEAD : (part + 1) * HEAD])
            return running

        running = lax.fori_loop(
            0, chunks, score, jnp.full((rows, HEAD), masked_fill, jnp.float32)
        )
        top = jnp.max(running, axis=1, keepdims=True)

        def mix(chunk, acc, top=top):
            start = pl.multiple_of(chunk * CHUNK, CHUNK)
            p = jnp.exp2((scores[chunk] - top) * exponent_scale).astype(jnp.bfloat16)
            return acc + jnp.dot(
                p, values[pl.ds(start, CHUNK), :], preferred_element_type=jnp.float32
            )

        acc = lax.fori_loop(0, chunks, mix, jnp.zeros((rows, 2 * HEAD), jnp.float32))
        total = acc[:, HEAD:]
        mixed = acc[:, :HEAD] / jnp.where(total > 0.0, total, 1.0)
        stats = jnp.zeros((STRETCH, HEAD), jnp.float32)
        where_row = slice(slot * STRETCH, (slot + 1) * STRETCH)
        for head in range(HEADS):
            span = slice(head * STRETCH, (head + 1) * STRETCH)
            out[peer, where_row, head * HEAD : (head + 1) * HEAD] = mixed[span].astype(
                jnp.bfloat16
            )
            for kind, whole in enumerate((jnp.broadcast_to(top[span], (STRETCH, HEAD)), total[span])):
                rest = whole
                for digit in range(3):
                    part = rest.astype(jnp.bfloat16).astype(jnp.float32)
                    stats = jnp.where(small_lane == head * 6 + kind * 3 + digit, part, stats)
                    rest = rest - part
        out[peer, where_row, HEADS * HEAD :] = stats.astype(jnp.bfloat16)


def combine_kernel(parts, out):
    stats = [parts[peer, :, HEADS * HEAD :].astype(jnp.float32) for peer in range(4)]
    for head in range(HEADS):
        tops = []
        totals = []
        for peer in range(4):
            column = [stats[peer][:, head * 6 + k : head * 6 + k + 1] for k in range(6)]
            tops.append(column[0] + column[1] + column[2])
            totals.append(column[3] + column[4] + column[5])
        top = jnp.maximum(jnp.maximum(tops[0], tops[1]), jnp.maximum(tops[2], tops[3]))
        weights = [jnp.exp2((tops[k] - top) * exponent_scale) * totals[k] for k in range(4)]
        whole = weights[0] + weights[1] + weights[2] + weights[3]
        mixed = 0.0
        for peer in range(4):
            share = jnp.broadcast_to(weights[peer] / whole, (ROWS, HEAD))
            mixed += share * parts[peer, :, head * HEAD : (head + 1) * HEAD].astype(jnp.float32)
        out[:, head * HEAD : (head + 1) * HEAD] = mixed.astype(jnp.bfloat16)


def on_device(tokens, stretch_table, query_weight, key_weight, value_weight):
    bf16, f32 = jnp.bfloat16, jnp.float32
    y = lax.axis_index("y")
    zl = lax.axis_index("zl")
    core = lax.axis_index("core")
    rows = tokens[0]
    sliced = lax.all_to_all(
        jnp.transpose(rows.reshape(ROWS, 4, 1024), (1, 0, 2)), "y", 0, 0
    ).reshape(4 * ROWS, 1024)
    own = jnp.concatenate([key_weight, value_weight, query_weight], axis=1)
    along_z = spread(own, ("zl", "zh"), 16)
    along_x = spread(along_z, "x", 4)
    across = swap(along_x, "core", 2, 1)
    both = jnp.where(core == 0, jnp.stack([along_x, across]), jnp.stack([across, along_x]))
    weight = jnp.transpose(both.reshape(2, 4, 8, 2, 8, 768), (2, 0, 3, 1, 4, 5)).reshape(1024, 768)

    table = stretch_table.reshape(4, 8, 2, 2)
    own_stretches = table[y, zl, core]
    offsets = jnp.arange(STRETCH, dtype=jnp.int32)
    positions = (own_stretches[:, None] * STRETCH + offsets[None, :]).reshape(ROWS)
    cosine, sine = angle_tables(positions)
    r = jnp.arange(16, dtype=jnp.int32)
    key_zl = zl ^ (4 * (r & 1)) ^ (2 * ((r >> 1) & 1)) ^ ((r >> 2) & 1)
    key_core = core ^ (r >> 3)
    key_index = y * 16 + key_zl * 2 + key_core
    device = jnp.arange(64, dtype=jnp.int32)
    pick = key_index[:, None, None] == device[None, :, None]
    key_stretch = jnp.sum(jnp.where(pick, stretch_table[None], 0), axis=1).reshape(32)
    query_index = jnp.arange(4, dtype=jnp.int32) * 16 + zl * 2 + core
    pick = query_index[:, None, None] == device[None, :, None]
    query_stretch = jnp.sum(jnp.where(pick, stretch_table[None], 0), axis=1).reshape(8)
    ranks = jnp.sum((key_stretch[None, :] < key_stretch[:, None]).astype(jnp.int32), axis=1)
    counts = jnp.sum((key_stretch[None, :] < query_stretch[:, None]).astype(jnp.int32), axis=1)
    plan = jnp.concatenate([ranks, counts, jnp.full((8,), y, jnp.int32)])

    part = jnp.dot(sliced, weight[:, : 2 * HEAD], preferred_element_type=f32)
    part = lax.all_to_all(part.reshape(4, ROWS, 2 * HEAD), "y", 0, 0)
    key_value = pl.pallas_call(
        key_value_kernel,
        out_shape=jax.ShapeDtypeStruct((ROWS, 2 * HEAD), bf16),
        in_specs=[vmem] * 3,
        out_specs=vmem,
        name="key_value",
    )(part, cosine, sine)

    step = swap(key_value, "zl", 8, 4)
    step = jnp.concatenate([key_value, step], axis=0)
    near = jnp.concatenate([step, swap(step, "zl", 8, 2)], axis=0)
    far = swap(near, "zl", 8, 1)
    other_near = swap(near, "core", 2, 1)
    other_far = swap(far, "core", 2, 1)

    part = jnp.dot(sliced, weight[:, 2 * HEAD :], preferred_element_type=f32)
    part = lax.all_to_all(part.reshape(4, ROWS, HEADS * HEAD), "y", 0, 0)
    query = pl.pallas_call(
        query_kernel,
        out_shape=jax.ShapeDtypeStruct((HEADS * ROWS, HEAD), bf16),
        in_specs=[vmem] * 3,
        out_specs=vmem,
        name="query",
    )(part, cosine, sine)
    query = spread(query, "y", 4).reshape(4 * HEADS * ROWS, HEAD)

    partial = pl.pallas_call(
        attention_kernel,
        out_shape=jax.ShapeDtypeStruct((4, ROWS, HEADS * HEAD + HEAD), bf16),
        in_specs=[smem] + [vmem] * 5,
        out_specs=vmem,
        scratch_shapes=[
            pltpu.VMEM((KEYS, HEAD), bf16),
            pltpu.VMEM((KEYS, 2 * HEAD), bf16),
            pltpu.VMEM((KEYS // CHUNK, HEADS * STRETCH, CHUNK), f32),
        ],
        name="attention",
    )(plan, query, near, far, other_near, other_far)
    partial = lax.all_to_all(partial, "y", 0, 0)
    attended = pl.pallas_call(
        combine_kernel,
        out_shape=jax.ShapeDtypeStruct((ROWS, HEADS * HEAD), bf16),
        in_specs=[vmem],
        out_specs=vmem,
        name="combine",
    )(partial)
    return attended[None]


def solution(mesh):
    fine = Mesh(mesh.devices.reshape(4, 8, 2, 2, 4), ("y", "zl", "core", "zh", "x"))
    ctx = ("y", "zl", "core")
    dp = ("zh", "x")
    placed = (
        P(dp, ctx, None),
        P(),
        P(ctx + dp, None),
        P(ctx + dp, None),
        P(ctx + dp, None),
    )
    return jax.shard_map(
        on_device, mesh=fine, in_specs=placed, out_specs=P(dp, ctx, None), check_vma=False
    )
```

time: 1500 us -> 160 us (0.11)
  the two profiles are of different devices: /device:TPU:19 before, /device:TPU:128 now
where the time goes in v1:
time: 160 us; the launch traced here: 159 us
  starting transfers between devices  47.4 us (30%)
  blocking collectives  38.5 us (24%)
  waiting for transfers between devices  34.5 us (22%)
  Pallas kernels  20 us (12%)
  local copies, waits for them, and re-layouts  10.4 us (6%)
  other arithmetic  5.32 us (3%)
  matrix products  2.19 us (1%)
    ppermute x6, starting transfers between devices, swap(): return lax.ppermute(value, axis, [(i, i ^ distance) for i in range(size)])  26.7 us
    all_to_all x1, blocking collectives, spread(): return lax.all_to_all(copies, axis, 0, 0)  24.3 us
    all_to_all x1, blocking collectives, on_device(): partial = lax.all_to_all(partial, 'y', 0, 0)  14.2 us
    pallas_call x1, Pallas kernels, on_device(): pl.pallas_call(attention_kernel, out_shape=jax.ShapeDtypeStruct((4, ROWS,...  13.8 us
    all_to_all x2, waiting for transfers between devices, spread(): return lax.all_to_all(copies, axis, 0, 0)  12.2 us
    all_to_all x2, starting transfers between devices, spread(): return lax.all_to_all(copies, axis, 0, 0)  9.31 us
    all_to_all x1, waiting for transfers between devices, on_device(): lax.all_to_all(jnp.transpose(rows.reshape(ROWS, 4, 1024), (1, 0, 2)), 'y'...  8.87 us
    ppermute x6, waiting for transfers between devices, swap(): return lax.ppermute(value, axis, [(i, i ^ distance) for i in range(size)])  7.18 us
  transfers between devices with their start and end apart: 11, of which 6 were waited for; matrix products, arithmetic and copies ran while one was open for 7% of the time, Pallas kernels for 2%

profile of v1, /device:TPU:128, one launch (start us, length us, event | category | flops | bytes accessed | tf_op | source)
XLA Modules:
  0.0 158.6 jit_solution(12073969688506437155)
XLA Ops:
  0.7 24.3 %all_to_all.35 = bf16[16,8,768]{2,1,0:T(8,128)(2,1)S(1)} all-to-all(bf16[16,8,768]{2,1,0:T(8,128)(2,1)S(1)} %broadcast_in_dim.80), channel_id=1, replica_groups=mesh['y'=4,'zl'=8,'core'=2,'zh'=2,'x'=4] {'zl','zh'}, dimensions={0} | all-to-all | bytes 393216 | tf_op jit(solution)/shard_map/all_to_all | solution.py:31
  26.0 4.3 %all-to-all-start.1 = ((bf16[4,16,8,768]{3,2,1,0:T(8,128)(2,1)}), bf16[4,16,8,768]{3,2,1,0:T(8,128)(2,1)S(1)}, u32[]{:S(2)}, u32[]{:S(2)}) async-start(bf16[4,16,8,768]{3,2,1,0:T(8,128)(2,1)} %broadcast_in_dim.81), calls=%async_computation.1 | async-start | bytes 1572864 | tf_op jit(solution)/shard_map/all_to_all | solution.py:31
  31.6 9.8 %all-to-all-done.1 = bf16[4,16,8,768]{3,2,1,0:T(8,128)(2,1)S(1)} async-done(((bf16[4,16,8,768]{3,2,1,0:T(8,128)(2,1)}), bf16[4,16,8,768]{3,2,1,0:T(8,128)(2,1)S(1)}, u32[]{:S(2)}, u32[]{:S(2)}) %all-to-all-start.1) | async-done | bytes 786464 | tf_op jit(solution)/shard_map/all_to_all | solution.py:31
  41.4 4.5 %all-to-all-start.2 = ((bf16[4,128,1024]{1,2,0:T(8,128)(2,1)}), bf16[4,128,1024]{1,2,0:T(8,128)(2,1)S(1)}, u32[]{:S(2)}, u32[]{:S(2)}) async-start(bf16[4,128,1024]{1,2,0:T(8,128)(2,1)} %bitcast.5), calls=%async_computation.2 | async-start | bytes 2097152 | tf_op jit(solution)/shard_map/all_to_all | solution.py:156
  45.9 1.9 %collective-permute-start = (bf16[4,16,8,768]{3,2,1,0:T(8,128)(2,1)S(1)}, bf16[4,16,8,768]{3,2,1,0:T(8,128)(2,1)}, u32[]{:S(2)}, u32[]{:S(2)}) collective-permute-start(bf16[4,16,8,768]{3,2,1,0:T(8,128)(2,1)S(1)} %all-to-all-done.1), channel_id=1, source_target_pairs={{0,8},{8,0},{1,9},{9,1},{2,10},{10,2},{3,11},{11,3},{4,12},{12,4},... | collective-permute-start | bytes 2359304 | tf_op jit(solution)/shard_map/ppermute | solution.py:26
  49.4 8.9 %all-to-all-done.2 = bf16[4,128,1024]{1,2,0:T(8,128)(2,1)S(1)} async-done(((bf16[4,128,1024]{1,2,0:T(8,128)(2,1)}), bf16[4,128,1024]{1,2,0:T(8,128)(2,1)S(1)}, u32[]{:S(2)}, u32[]{:S(2)}) %all-to-all-start.2) | async-done | bytes 1048608 | tf_op jit(solution)/shard_map/all_to_all | solution.py:156
  62.9 3.5 %all-to-all-start.5 = ((f32[4,128,256]{2,1,0:T(8,128)}), f32[4,128,256]{2,1,0:T(8,128)S(1)}, u32[]{:S(2)}, u32[]{:S(2)}) async-start(f32[4,128,256]{2,1,0:T(8,128)} %bitcast.28), calls=%async_computation.5 | async-start | bytes 1048576 | tf_op jit(solution)/shard_map/all_to_all | solution.py:186
  68.1 6.3 %all-to-all-done.5.parts = f32[4,128,256]{2,1,0:T(8,128)S(1)} async-done(((f32[4,128,256]{2,1,0:T(8,128)}), f32[4,128,256]{2,1,0:T(8,128)S(1)}, u32[]{:S(2)}, u32[]{:S(2)}) %all-to-all-start.5) | async-done | bytes 524320 | tf_op jit(solution)/shard_map/all_to_all | solution.py:186
  74.5 3.5 %all-to-all-start.3 = ((f32[4,128,512]{2,1,0:T(8,128)}), f32[4,128,512]{2,1,0:T(8,128)S(1)}, u32[]{:S(2)}, u32[]{:S(2)}) async-start(f32[4,128,512]{2,1,0:T(8,128)} %bitcast.29), calls=%async_computation.3 | async-start | bytes 2097152 | tf_op jit(solution)/shard_map/all_to_all | solution.py:203
  78.0 1.8 %key_value.1 = bf16[128,256]{1,0:T(8,128)(2,1)} custom-call(f32[4,128,256]{2,1,0:T(8,128)} %copy-done.4, f32[128,128]{1,0:T(8,128)} %get-tuple-element.8.cosine, f32[128,128]{1,0:T(8,128)} %get-tuple-element.9.sine), custom_call_target="tpu_custom_call" | custom-call | tf_op jit(solution)/shard_map/key_value/pallas_call | solution.py:187
  79.8 6.2 %collective-permute-start.1 = (bf16[128,256]{1,0:T(8,128)(2,1)}, bf16[128,256]{1,0:T(8,128)(2,1)S(1)}, u32[]{:S(2)}, u32[]{:S(2)}) collective-permute-start(bf16[128,256]{1,0:T(8,128)(2,1)} %key_value.1), channel_id=1, source_target_pairs={{0,64},{16,80},{32,96},{48,112},{64,0},{80,16},{96,32},{112,48},{1... | collective-permute-start | bytes 196616 | tf_op jit(solution)/shard_map/ppermute | solution.py:26
  86.1 4.1 %collective-permute-done.1 = bf16[128,256]{1,0:T(8,128)(2,1)S(1)} collective-permute-done((bf16[128,256]{1,0:T(8,128)(2,1)}, bf16[128,256]{1,0:T(8,128)(2,1)S(1)}, u32[]{:S(2)}, u32[]{:S(2)}) %collective-permute-start.1) | collective-permute-done | bytes 65568 | tf_op jit(solution)/shard_map/ppermute | solution.py:26
  91.0 5.9 %collective-permute-start.2 = (bf16[256,256]{1,0:T(8,128)(2,1)S(1)}, bf16[256,256]{1,0:T(8,128)(2,1)S(1)}, u32[]{:S(2)}, u32[]{:S(2)}) collective-permute-start(bf16[256,256]{1,0:T(8,128)(2,1)S(1)} %pad_maximum_fusion.1), channel_id=1, source_target_pairs={{0,32},{16,48},{32,0},{48,16},{64,96},{80,112},{96,64},{112,80},{1... | collective-permute-start | bytes 393224 | tf_op jit(solution)/shard_map/ppermute | solution.py:26
  97.3 3.1 %collective-permute-done.2 = bf16[256,256]{1,0:T(8,128)(2,1)S(1)} collective-permute-done((bf16[256,256]{1,0:T(8,128)(2,1)S(1)}, bf16[256,256]{1,0:T(8,128)(2,1)S(1)}, u32[]{:S(2)}, u32[]{:S(2)}) %collective-permute-start.2) | collective-permute-done | bytes 131104 | tf_op jit(solution)/shard_map/ppermute | solution.py:26
  101.2 8.3 %collective-permute-start.3 = (bf16[512,256]{1,0:T(8,128)(2,1)S(1)}, bf16[512,256]{1,0:T(8,128)(2,1)S(1)}, u32[]{:S(2)}, u32[]{:S(2)}) collective-permute-start(bf16[512,256]{1,0:T(8,128)(2,1)S(1)} %pad_maximum_fusion.own_near), channel_id=1, source_target_pairs={{0,16},{16,0},{32,48},{48,32},{64,80},{80,64},{96,112},{112,96},{1... | collective-permute-start | bytes 786440 | tf_op jit(solution)/shard_map/ppermute | solution.py:26
  110.6 2.1 %query.1 = bf16[512,128]{1,0:T(8,128)(2,1)} custom-call(f32[4,128,512]{2,1,0:T(8,128)} %copy-done, f32[128,128]{1,0:T(8,128)} %get-tuple-element.8.cosine, f32[128,128]{1,0:T(8,128)} %get-tuple-element.9.sine), custom_call_target="tpu_custom_call" | custom-call | tf_op jit(solution)/shard_map/query/pallas_call | solution.py:204
  112.7 1.8 %broadcast_in_dim.82 = bf16[4,512,128]{2,1,0:T(8,128)(2,1)} broadcast(bf16[512,128]{1,0:T(8,128)(2,1)} %query.1), dimensions={1,2} | broadcast | bytes 655360 | tf_op jit(solution)/shard_map/broadcast_in_dim | solution.py:30
  114.4 5.0 %all-to-all-start.4 = ((bf16[4,512,128]{2,1,0:T(8,128)(2,1)}), bf16[4,512,128]{2,1,0:T(8,128)(2,1)S(1)}, u32[]{:S(2)}, u32[]{:S(2)}) async-start(bf16[4,512,128]{2,1,0:T(8,128)(2,1)} %broadcast_in_dim.82), calls=%async_computation.4 | async-start | bytes 1048576 | tf_op jit(solution)/shard_map/all_to_all | solution.py:31
  119.6 1.9 %collective-permute-start.4 = (bf16[512,256]{1,0:T(8,128)(2,1)S(1)}, bf16[512,256]{1,0:T(8,128)(2,1)S(1)}, u32[]{:S(2)}, u32[]{:S(2)}) collective-permute-start(bf16[512,256]{1,0:T(8,128)(2,1)S(1)} %pad_maximum_fusion.own_near), channel_id=1, source_target_pairs={{0,8},{8,0},{1,9},{9,1},{2,10},{10,2},{3,11},{11,3},{4,12},{12,4},... | collective-permute-start | bytes 786440 | tf_op jit(solution)/shard_map/ppermute | solution.py:26
  121.6 2.4 %collective-permute-start.5 = (bf16[512,256]{1,0:T(8,128)(2,1)S(1)}, bf16[512,256]{1,0:T(8,128)(2,1)S(1)}, u32[]{:S(2)}, u32[]{:S(2)}) collective-permute-start(bf16[512,256]{1,0:T(8,128)(2,1)S(1)} %collective-permute-done.3.own_far), channel_id=1, source_target_pairs={{0,8},{8,0},{1,9},{9,1},{2,10},{10,2},{3,11},{11,3},{4,12},{12,4},... | collective-permute-start | bytes 786440 | tf_op jit(solution)/shard_map/ppermute | solution.py:26
  125.1 2.4 %all-to-all-done.4 = bf16[4,512,128]{2,1,0:T(8,128)(2,1)S(1)} async-done(((bf16[4,512,128]{2,1,0:T(8,128)(2,1)}), bf16[4,512,128]{2,1,0:T(8,128)(2,1)S(1)}, u32[]{:S(2)}, u32[]{:S(2)}) %all-to-all-start.4) | async-done | bytes 524320 | tf_op jit(solution)/shard_map/all_to_all | solution.py:31
  128.3 13.8 %attention.1 = bf16[4,128,640]{2,1,0:T(8,128)(2,1)} custom-call(s32[48]{0:T(128)} %pad_add_fusion.plan, bf16[2048,128]{1,0:T(8,128)(2,1)} %bitcast.27, bf16[512,256]{1,0:T(8,128)(2,1)} %copy-done.5, bf16[512,256]{1,0:T(8,128)(2,1)} %copy-done.7, bf16[512,256]{1,0:T(8,128)(2,1)} %copy-done.8, bf16[512,256]{1,0:T(8,128)(2,1)} %copy-done.9), custom_call_target="tpu_custom_call" | custom-call | tf_op jit(solution)/shard_map/attention/pallas_call | solution.py:213
  142.1 14.2 %all_to_all.36.parts = bf16[4,128,640]{2,1,0:T(8,128)(2,1)} all-to-all(bf16[4,128,640]{2,1,0:T(8,128)(2,1)} %attention.1), channel_id=1, replica_groups=mesh['y'=4,'zl'=8,'core'=2,'zh'=2,'x'=4] {'y'}, dimensions={0} | all-to-all | bytes 1310720 | tf_op jit(solution)/shard_map/all_to_all | solution.py:225
  156.3 2.3 %combine.1 = bf16[128,512]{1,0:T(8,128)(2,1)} custom-call(bf16[4,128,640]{2,1,0:T(8,128)(2,1)} %all_to_all.36.parts), custom_call_target="tpu_custom_call" | custom-call | tf_op jit(solution)/shard_map/combine/pallas_call | solution.py:226
  (61 shorter events, 16.2 us)
Async XLA Ops:
  0.7 29.6 %copy-start.6 = (bf16[1,128,4096]{2,1,0:T(8,128)(2,1)S(1)}, bf16[1,128,4096]{2,1,0:T(8,128)(2,1)}, u32[]{:S(2)}) copy-start(bf16[1,128,4096]{2,1,0:T(8,128)(2,1)} %param.5) | copy-start | bytes 3145732
  26.0 15.4 %all-to-all-start.1 = ((bf16[4,16,8,768]{3,2,1,0:T(8,128)(2,1)}), bf16[4,16,8,768]{3,2,1,0:T(8,128)(2,1)S(1)}, u32[]{:S(2)}, u32[]{:S(2)}) async-start(bf16[4,16,8,768]{3,2,1,0:T(8,128)(2,1)} %broadcast_in_dim.81), calls=%async_computation.1 | async-start | bytes 1572864 | tf_op jit(solution)/shard_map/all_to_all | solution.py:31
  31.6 16.1 %copy-start.10 = (s32[64,2]{0,1:T(2,128)S(1)}, s32[64,2]{0,1:T(2,128)}, u32[]{:S(2)}) copy-start(s32[64,2]{0,1:T(2,128)} %param.6) | copy-start | bytes 1540
  41.4 16.8 %all-to-all-start.2 = ((bf16[4,128,1024]{1,2,0:T(8,128)(2,1)}), bf16[4,128,1024]{1,2,0:T(8,128)(2,1)S(1)}, u32[]{:S(2)}, u32[]{:S(2)}) async-start(bf16[4,128,1024]{1,2,0:T(8,128)(2,1)} %bitcast.5), calls=%async_computation.2 | async-start | bytes 2097152 | tf_op jit(solution)/shard_map/all_to_all | solution.py:156
  45.9 13.0 %collective-permute-start = (bf16[4,16,8,768]{3,2,1,0:T(8,128)(2,1)S(1)}, bf16[4,16,8,768]{3,2,1,0:T(8,128)(2,1)}, u32[]{:S(2)}, u32[]{:S(2)}) collective-permute-start(bf16[4,16,8,768]{3,2,1,0:T(8,128)(2,1)S(1)} %all-to-all-done.1), channel_id=1, source_target_pairs={{0,8},{8,0},{1,9},{9,1},{2,10},{10,2},{3,11},{11,3},{4,12},{12,4},... | collective-permute-start | bytes 2359304 | tf_op jit(solution)/shard_map/ppermute | solution.py:26
  60.2 1.2 copy-start.1
  61.9 4.5 %copy-start.2 = (bf16[2,4,8,2,8,768]{5,4,1,3,0,2:T(8,128)(2,1)S(1)}, bf16[2,4,8,2,8,768]{5,4,1,3,0,2:T(8,128)(2,1)}, u32[]{:S(2)}) copy-start(bf16[2,4,8,2,8,768]{5,4,1,3,0,2:T(8,128)(2,1)} %copy-done.1) | copy-start | bytes 4718596
  62.9 11.5 %all-to-all-start.5 = ((f32[4,128,256]{2,1,0:T(8,128)}), f32[4,128,256]{2,1,0:T(8,128)S(1)}, u32[]{:S(2)}, u32[]{:S(2)}) async-start(f32[4,128,256]{2,1,0:T(8,128)} %bitcast.28), calls=%async_computation.5 | async-start | bytes 1048576 | tf_op jit(solution)/shard_map/all_to_all | solution.py:186
  74.5 3.5 %copy-start.4 = (f32[4,128,256]{2,1,0:T(8,128)}, f32[4,128,256]{2,1,0:T(8,128)S(1)}, u32[]{:S(2)}) copy-start(f32[4,128,256]{2,1,0:T(8,128)S(1)} %all-to-all-done.5.parts) | copy-start | bytes 1572868
  74.5 35.1 %all-to-all-start.3 = ((f32[4,128,512]{2,1,0:T(8,128)}), f32[4,128,512]{2,1,0:T(8,128)S(1)}, u32[]{:S(2)}, u32[]{:S(2)}) async-start(f32[4,128,512]{2,1,0:T(8,128)} %bitcast.29), calls=%async_computation.3 | async-start | bytes 2097152 | tf_op jit(solution)/shard_map/all_to_all | solution.py:203
  79.8 10.4 %collective-permute-start.1 = (bf16[128,256]{1,0:T(8,128)(2,1)}, bf16[128,256]{1,0:T(8,128)(2,1)S(1)}, u32[]{:S(2)}, u32[]{:S(2)}) collective-permute-start(bf16[128,256]{1,0:T(8,128)(2,1)} %key_value.1), channel_id=1, source_target_pairs={{0,64},{16,80},{32,96},{48,112},{64,0},{80,16},{96,32},{112,48},{1... | collective-permute-start | bytes 196616 | tf_op jit(solution)/shard_map/ppermute | solution.py:26
  91.0 9.3 %collective-permute-start.2 = (bf16[256,256]{1,0:T(8,128)(2,1)S(1)}, bf16[256,256]{1,0:T(8,128)(2,1)S(1)}, u32[]{:S(2)}, u32[]{:S(2)}) collective-permute-start(bf16[256,256]{1,0:T(8,128)(2,1)S(1)} %pad_maximum_fusion.1), channel_id=1, source_target_pairs={{0,32},{16,48},{32,0},{48,16},{64,96},{80,112},{96,64},{112,80},{1... | collective-permute-start | bytes 393224 | tf_op jit(solution)/shard_map/ppermute | solution.py:26
  101.2 26.3 %copy-start.5 = (bf16[512,256]{1,0:T(8,128)(2,1)}, bf16[512,256]{1,0:T(8,128)(2,1)S(1)}, u32[]{:S(2)}) copy-start(bf16[512,256]{1,0:T(8,128)(2,1)S(1)} %pad_maximum_fusion.own_near) | copy-start | bytes 786436
  101.2 20.4 %collective-permute-start.3 = (bf16[512,256]{1,0:T(8,128)(2,1)S(1)}, bf16[512,256]{1,0:T(8,128)(2,1)S(1)}, u32[]{:S(2)}, u32[]{:S(2)}) collective-permute-start(bf16[512,256]{1,0:T(8,128)(2,1)S(1)} %pad_maximum_fusion.own_near), channel_id=1, source_target_pairs={{0,16},{16,0},{32,48},{48,32},{64,80},{80,64},{96,112},{112,96},{1... | collective-permute-start | bytes 786440 | tf_op jit(solution)/shard_map/ppermute | solution.py:26
  109.6 1.0 copy-start
  114.4 13.1 %all-to-all-start.4 = ((bf16[4,512,128]{2,1,0:T(8,128)(2,1)}), bf16[4,512,128]{2,1,0:T(8,128)(2,1)S(1)}, u32[]{:S(2)}, u32[]{:S(2)}) async-start(bf16[4,512,128]{2,1,0:T(8,128)(2,1)} %broadcast_in_dim.82), calls=%async_computation.4 | async-start | bytes 1048576 | tf_op jit(solution)/shard_map/all_to_all | solution.py:31
  119.6 5.5 %collective-permute-start.4 = (bf16[512,256]{1,0:T(8,128)(2,1)S(1)}, bf16[512,256]{1,0:T(8,128)(2,1)S(1)}, u32[]{:S(2)}, u32[]{:S(2)}) collective-permute-start(bf16[512,256]{1,0:T(8,128)(2,1)S(1)} %pad_maximum_fusion.own_near), channel_id=1, source_target_pairs={{0,8},{8,0},{1,9},{9,1},{2,10},{10,2},{3,11},{11,3},{4,12},{12,4},... | collective-permute-start | bytes 786440 | tf_op jit(solution)/shard_map/ppermute | solution.py:26
  121.5 6.0 %copy-start.7 = (bf16[512,256]{1,0:T(8,128)(2,1)}, bf16[512,256]{1,0:T(8,128)(2,1)S(1)}, u32[]{:S(2)}) copy-start(bf16[512,256]{1,0:T(8,128)(2,1)S(1)} %collective-permute-done.3.own_far) | copy-start | bytes 786436
  121.6 3.6 %collective-permute-start.5 = (bf16[512,256]{1,0:T(8,128)(2,1)S(1)}, bf16[512,256]{1,0:T(8,128)(2,1)S(1)}, u32[]{:S(2)}, u32[]{:S(2)}) collective-permute-start(bf16[512,256]{1,0:T(8,128)(2,1)S(1)} %collective-permute-done.3.own_far), channel_id=1, source_target_pairs={{0,8},{8,0},{1,9},{9,1},{2,10},{10,2},{3,11},{11,3},{4,12},{12,4},... | collective-permute-start | bytes 786440 | tf_op jit(solution)/shard_map/ppermute | solution.py:26
  125.1 2.4 %copy-start.8 = (bf16[512,256]{1,0:T(8,128)(2,1)}, bf16[512,256]{1,0:T(8,128)(2,1)S(1)}, u32[]{:S(2)}) copy-start(bf16[512,256]{1,0:T(8,128)(2,1)S(1)} %collective-permute-done.4.other_near) | copy-start | bytes 786436
  125.1 2.4 %copy-start.9 = (bf16[512,256]{1,0:T(8,128)(2,1)}, bf16[512,256]{1,0:T(8,128)(2,1)S(1)}, u32[]{:S(2)}) copy-start(bf16[512,256]{1,0:T(8,128)(2,1)S(1)} %collective-permute-done.5.other_far) | copy-start | bytes 786436
  127.5 0.8 copy-start.3

commit v2 on v1

v2 whole, which is shorter than its diff:
```python
import math

import jax
import jax.numpy as jnp
from jax import lax
from jax.experimental import pallas as pl
from jax.experimental.pallas import tpu as pltpu
from jax.sharding import Mesh, PartitionSpec as P

rope_base = 500000.0
masked_fill = -1e30
HEAD = 128
HEADS = 4
STRETCH = 64
ROWS = 128
KEYS = 2048
CHUNK = 512
score_scale = 1.0 / math.sqrt(HEAD)
exponent_scale = score_scale * math.log2(math.e)

vmem = pl.BlockSpec(memory_space=pltpu.VMEM)
smem = pl.BlockSpec(memory_space=pltpu.SMEM)


def swap(value, axis, size, distance):
    return lax.ppermute(value, axis, [(i, i ^ distance) for i in range(size)])


def spread(value, axis, size):
    copies = jnp.broadcast_to(value[None], (size,) + value.shape)
    return lax.all_to_all(copies, axis, 0, 0)


def angle_tables(positions):
    half = HEAD // 2
    frequency = rope_base ** (-(jnp.arange(half, dtype=jnp.float32) * 2.0 / HEAD))
    angles = positions.astype(jnp.float32)[:, None] * frequency[None, :]
    cosine = jnp.cos(angles)
    sine = jnp.sin(angles)
    return (
        jnp.concatenate([cosine, cosine], axis=1),
        jnp.concatenate([-sine, sine], axis=1),
    )


def key_value_kernel(parts, cosine, sine, out):
    total = parts[0] + parts[1] + parts[2] + parts[3]
    key = total[:, :HEAD]
    turned = key * cosine[...] + pltpu.roll(key, HEAD // 2, 1) * sine[...]
    out[:, :HEAD] = turned.astype(jnp.bfloat16)
    out[:, HEAD:] = total[:, HEAD:].astype(jnp.bfloat16)


def query_kernel(flip, parts, cosine, sine, out):
    for head in range(HEADS):
        span = slice(head * HEAD, (head + 1) * HEAD)
        total = parts[0, :, span] + parts[1, :, span] + parts[2, :, span] + parts[3, :, span]
        turned = total * cosine[...] + pltpu.roll(total, HEAD // 2, 1) * sine[...]
        turned = turned.astype(jnp.bfloat16)
        for slot in range(2):
            level = slot ^ flip[0]
            row = pl.multiple_of((level * HEADS + head) * STRETCH, STRETCH)
            piece = turned[slot * STRETCH : (slot + 1) * STRETCH]
            for copy in range(4):
                out[copy, pl.ds(row, STRETCH), :] = piece


def project_kernel(where, rows0, rows1, rows2, rows3, mine, across, out, weight):
    y = where[0]
    core = where[1]
    width = out.shape[2]
    first = 0 if width == 2 * HEAD else 2 * HEAD
    for far, source in enumerate((mine, across)):
        base = (core ^ far) * 64
        for group in range(8):
            for half in range(2):
                rows = [
                    source[x, (group * 2 + half) * 8 : (group * 2 + half) * 8 + 8, first : first + width]
                    for x in range(4)
                ]
                target = pl.multiple_of(group * 128 + half * 32 + base, 32)
                weight[pl.ds(target, 32), :] = jnp.concatenate(rows, axis=0)
    for shift, rows in enumerate((rows0, rows1, rows2, rows3)):
        out[(y + 4 - shift) % 4] = jnp.dot(
            rows[...], weight[...], preferred_element_type=jnp.float32
        )


def order_kernel(plan, own_near, own_far, other_near, other_far, keys, values):
    pieces = (own_near, own_far, other_near, other_far)
    values[:, HEAD:] = jnp.ones((KEYS, HEAD), jnp.bfloat16)
    for index in range(KEYS // STRETCH):
        piece = pieces[index // 8]
        source = (index % 8) * STRETCH
        target = pl.multiple_of(plan[index] * STRETCH, STRETCH)
        keys[pl.ds(target, STRETCH), :] = piece[source : source + STRETCH, :HEAD]
        values[pl.ds(target, STRETCH), :HEAD] = piece[source : source + STRETCH, HEAD:]


def scores_of(q, keys, low_key):
    return lax.dot_general(
        q, keys[low_key : low_key + CHUNK, :], (((1,), (1,)), ((), ())),
        preferred_element_type=jnp.float32,
    )


def attend_peer(plan, peer, q_low, q_high, keys, values, scores, write):
    rows = HEADS * STRETCH
    here = (plan[40] == peer).astype(jnp.int32)
    in_stretch = lax.broadcasted_iota(jnp.int32, (rows, HEAD), 0) % STRETCH + 1
    lane = lax.broadcasted_iota(jnp.int32, (rows, HEAD), 1)
    slack = in_stretch * here - lane
    small_lane = lax.broadcasted_iota(jnp.int32, (STRETCH, HEAD), 1)
    tops = []
    for level, q in enumerate((q_low, q_high)):
        full = (plan[32 + 2 * peer + level] - 16 * level) * STRETCH
        running = jnp.full((rows, HEAD), -1e20, jnp.float32)
        for block in range(2 * (1 + level)):
            masked = level == 0 or block >= 2
            s = scores_of(q, keys, block * CHUNK)
            for part in range(CHUNK // HEAD):
                lanes = slice(part * HEAD, (part + 1) * HEAD)
                t = s[:, lanes]
                if masked:
                    start = (block % 2) * CHUNK + part * HEAD
                    t = jnp.where(slack > start - full, t, masked_fill)
                scores[2 * level + block, :, lanes] = t
                running = jnp.maximum(running, t)
        tops.append(jnp.max(running, axis=1, keepdims=True))
    for level in range(2):
        top = tops[level]
        acc = jnp.zeros((rows, 2 * HEAD), jnp.float32)
        for block in range(2 * (1 + level)):
            p = jnp.exp2((scores[2 * level + block] - top) * exponent_scale).astype(jnp.bfloat16)
            acc = acc + jnp.dot(
                p, values[block * CHUNK : (block + 1) * CHUNK, :], preferred_element_type=jnp.float32
            )
        total = acc[:, HEAD:]
        mixed = acc[:, :HEAD] / jnp.where(total > 0.0, total, 1.0)
        stats = jnp.zeros((STRETCH, HEAD), jnp.float32)
        row = pl.multiple_of((level ^ plan[41 + peer]) * STRETCH, STRETCH)
        for head in range(HEADS):
            span = slice(head * STRETCH, (head + 1) * STRETCH)
            write(row, slice(head * HEAD, (head + 1) * HEAD), mixed[span].astype(jnp.bfloat16))
            for kind, whole in enumerate((jnp.broadcast_to(top[span], (STRETCH, HEAD)), total[span])):
                rest = whole
                for digit in range(3):
                    part = rest.astype(jnp.bfloat16).astype(jnp.float32)
                    stats = jnp.where(small_lane == head * 6 + kind * 3 + digit, part, stats)
                    rest = rest - part
        write(row, slice(HEADS * HEAD, HEADS * HEAD + HEAD), stats.astype(jnp.bfloat16))


def peers_kernel(plan, query, keys, values, out, scores):
    rows = HEADS * STRETCH
    own = plan[40]
    out[own] = jnp.zeros(out.shape[1:], jnp.bfloat16)

    def body(shift, carried):
        peer = (own + shift) % 4

        def write(row, lanes, value):
            out[peer, pl.ds(row, STRETCH), lanes] = value

        attend_peer(
            plan, peer, query[peer, :rows, :], query[peer, rows:, :], keys, values, scores, write
        )
        return carried

    lax.fori_loop(1, 4, body, 0)


def own_kernel(plan, query, keys, values, out, scores):
    rows = HEADS * STRETCH

    def write(row, lanes, value):
        out[pl.ds(row, STRETCH), lanes] = value

    attend_peer(
        plan, plan[40], query[0, :rows, :], query[0, rows:, :], keys, values, scores, write
    )


def combine_kernel(plan, parts, own, out):
    y = plan[40]
    lane = lax.broadcasted_iota(jnp.int32, (HEAD, 8 * HEAD), 0)
    group = lax.broadcasted_iota(jnp.int32, (HEAD, 8 * HEAD), 1) // HEAD
    pick = (lane // 3 == group).astype(jnp.float32).astype(jnp.bfloat16)
    results = [jnp.where(y == peer, own[...], parts[peer]) for peer in range(4)]
    spread_stats = [
        jnp.dot(result[:, HEADS * HEAD :], pick, preferred_element_type=jnp.float32)
        for result in results
    ]
    for head in range(HEADS):
        tops = [w[:, 2 * head * HEAD : (2 * head + 1) * HEAD] for w in spread_stats]
        totals = [w[:, (2 * head + 1) * HEAD : (2 * head + 2) * HEAD] for w in spread_stats]
        top = jnp.maximum(jnp.maximum(tops[0], tops[1]), jnp.maximum(tops[2], tops[3]))
        weights = [jnp.exp2((tops[k] - top) * exponent_scale) * totals[k] for k in range(4)]
        whole = weights[0] + weights[1] + weights[2] + weights[3]
        mixed = 0.0
        for peer in range(4):
            mixed += weights[peer] * results[peer][:, head * HEAD : (head + 1) * HEAD].astype(jnp.float32)
        out[:, head * HEAD : (head + 1) * HEAD] = (mixed / whole).astype(jnp.bfloat16)


def after(value, *others):
    return lax.optimization_barrier((value,) + others)[0]


def on_device(tokens, stretch_table, query_weight, key_weight, value_weight):
    bf16, f32 = jnp.bfloat16, jnp.float32
    y = lax.axis_index("y")
    zl = lax.axis_index("zl")
    core = lax.axis_index("core")
    rows = tokens[0]
    own = jnp.concatenate([key_weight, value_weight, query_weight], axis=1)
    along_z = spread(own, ("zl", "zh"), 16)
    sliced = []
    for shift in range(4):
        target = (y + shift) % 4
        piece = lax.dynamic_slice_in_dim(rows, target * 1024, 1024, 1)
        if shift:
            piece = lax.ppermute(piece, "y", [(i, (i + shift) % 4) for i in range(4)])
        sliced.append(piece)
    along_z = after(along_z, *sliced)
    along_x = spread(along_z, "x", 4).reshape(4, ROWS, 768)
    across = swap(along_x, "core", 2, 1)

    table = stretch_table.reshape(4, 8, 2, 2)
    own_stretches = table[y, zl, core]
    offsets = jnp.arange(STRETCH, dtype=jnp.int32)
    positions = (own_stretches[:, None] * STRETCH + offsets[None, :]).reshape(ROWS)
    cosine, sine = angle_tables(positions)
    r = jnp.arange(16, dtype=jnp.int32)
    key_zl = zl ^ (4 * (r & 1)) ^ (2 * ((r >> 1) & 1)) ^ ((r >> 2) & 1)
    key_core = core ^ (r >> 3)
    key_index = y * 16 + key_zl * 2 + key_core
    device = jnp.arange(64, dtype=jnp.int32)
    pick = key_index[:, None, None] == device[None, :, None]
    key_stretch = jnp.sum(jnp.where(pick, stretch_table[None], 0), axis=1).reshape(32)
    query_index = jnp.arange(4, dtype=jnp.int32) * 16 + zl * 2 + core
    pick = query_index[:, None, None] == device[None, :, None]
    query_stretch = jnp.sum(jnp.where(pick, stretch_table[None], 0), axis=1)
    flips = (query_stretch[:, 0] > query_stretch[:, 1]).astype(jnp.int32)
    levels = jnp.stack(
        [jnp.min(query_stretch, axis=1), jnp.max(query_stretch, axis=1)], axis=1
    ).reshape(8)
    ranks = jnp.sum((key_stretch[None, :] < key_stretch[:, None]).astype(jnp.int32), axis=1)
    counts = jnp.sum((key_stretch[None, :] < levels[:, None]).astype(jnp.int32), axis=1)
    plan = jnp.concatenate([ranks, counts, y[None].astype(jnp.int32), flips])
    where = jnp.stack([y, core]).astype(jnp.int32)
    flip = (own_stretches[:1] > own_stretches[1:]).astype(jnp.int32)

    def project(width, across):
        part = pl.pallas_call(
            project_kernel,
            out_shape=jax.ShapeDtypeStruct((4, ROWS, width), f32),
            in_specs=[smem] + [vmem] * 6,
            out_specs=vmem,
            scratch_shapes=[pltpu.VMEM((1024, width), bf16)],
            name="project",
        )(where, *sliced, along_x, across)
        return part

    part = project(2 * HEAD, across)
    query_part = project(HEADS * HEAD, after(across, part))
    part = lax.all_to_all(part, "y", 0, 0)
    key_value = pl.pallas_call(
        key_value_kernel,
        out_shape=jax.ShapeDtypeStruct((ROWS, 2 * HEAD), bf16),
        in_specs=[vmem] * 3,
        out_specs=vmem,
        name="key_value",
    )(part, cosine, sine)
    query_part = lax.all_to_all(after(query_part, key_value), "y", 0, 0)

    step = swap(key_value, "zl", 8, 4)
    step = jnp.concatenate([key_value, step], axis=0)
    near = jnp.concatenate([step, swap(step, "zl", 8, 2)], axis=0)
    far = swap(near, "zl", 8, 1)
    other_near = swap(near, "core", 2, 1)
    other_far = swap(far, "core", 2, 1)

    query = pl.pallas_call(
        query_kernel,
        out_shape=jax.ShapeDtypeStruct((4, HEADS * ROWS, HEAD), bf16),
        in_specs=[smem] + [vmem] * 3,
        out_specs=vmem,
        name="query",
    )(flip, query_part, cosine, sine)
    queries = lax.all_to_all(query, "y", 0, 0)

    keys, values = pl.pallas_call(
        order_kernel,
        out_shape=(
            jax.ShapeDtypeStruct((KEYS, HEAD), bf16),
            jax.ShapeDtypeStruct((KEYS, 2 * HEAD), bf16),
        ),
        in_specs=[smem] + [vmem] * 4,
        out_specs=(vmem, vmem),
        name="order",
    )(plan, near, far, other_near, other_far)
    score_scratch = [pltpu.VMEM((6, HEADS * STRETCH, CHUNK), f32)]
    partial = pl.pallas_call(
        peers_kernel,
        out_shape=jax.ShapeDtypeStruct((4, ROWS, HEADS * HEAD + HEAD), bf16),
        in_specs=[smem] + [vmem] * 3,
        out_specs=vmem,
        scratch_shapes=score_scratch,
        name="peers",
    )(plan, queries, keys, values)
    own_partial = pl.pallas_call(
        own_kernel,
        out_shape=jax.ShapeDtypeStruct((ROWS, HEADS * HEAD + HEAD), bf16),
        in_specs=[smem] + [vmem] * 3,
        out_specs=vmem,
        scratch_shapes=score_scratch,
        name="own",
    )(plan, after(query, partial), keys, values)
    partial = lax.all_to_all(partial, "y", 0, 0)
    attended = pl.pallas_call(
        combine_kernel,
        out_shape=jax.ShapeDtypeStruct((ROWS, HEADS * HEAD), bf16),
        in_specs=[smem] + [vmem] * 2,
        out_specs=vmem,
        name="combine",
    )(plan, partial, own_partial)
    return attended[None]


def solution(mesh):
    fine = Mesh(mesh.devices.reshape(4, 8, 2, 2, 4), ("y", "zl", "core", "zh", "x"))
    ctx = ("y", "zl", "core")
    dp = ("zh", "x")
    placed = (
        P(dp, ctx, None),
        P(),
        P(ctx + dp, None),
        P(ctx + dp, None),
        P(ctx + dp, None),
    )
    return jax.shard_map(
        on_device, mesh=fine, in_specs=placed, out_specs=P(dp, ctx, None), check_vma=False
    )
```

time: 160 us -> 151 us (0.944)
  the two profiles are of different devices: /device:TPU:128 before, /device:TPU:64 now
where the time goes in v2:
time: 151 us; the launch traced here: 150 us
  starting transfers between devices  72.5 us (48%)
  waiting for transfers between devices  34.5 us (23%)
  Pallas kernels  26.6 us (18%)
  local copies, waits for them, and re-layouts  11.1 us (7%)
  other arithmetic  4.13 us (3%)
    ppermute x6, starting transfers between devices, swap(): return lax.ppermute(value, axis, [(i, i ^ distance) for i in range(size)])  24.3 us
    all_to_all x2, starting transfers between devices, spread(): return lax.all_to_all(copies, axis, 0, 0)  19.1 us
    ppermute x3, starting transfers between devices, on_device(): piece = lax.ppermute(piece, 'y', [(i, (i + shift) % 4) for i in range(4)])  11.5 us
    all_to_all x2, waiting for transfers between devices, spread(): return lax.all_to_all(copies, axis, 0, 0)  9.84 us
    all_to_all x1, waiting for transfers between devices, on_device(): partial = lax.all_to_all(partial, 'y', 0, 0)  7.29 us
    ppermute x3, waiting for transfers between devices, on_device(): piece = lax.ppermute(piece, 'y', [(i, (i + shift) % 4) for i in range(4)])  7.18 us
    pallas_call x1, Pallas kernels, on_device(): pl.pallas_call(peers_kernel, out_shape=jax.ShapeDtypeStruct((4, ROWS, HEA...  7.1 us
    pallas_call x2, Pallas kernels, project(): pl.pallas_call(project_kernel, out_shape=jax.ShapeDtypeStruct((4, ROWS, w...  6.61 us
  transfers between devices with their start and end apart: 15, of which 8 were waited for; matrix products, arithmetic and copies ran while one was open for 4% of the time, Pallas kernels for 8%

profile of v2, /device:TPU:64, one launch (start us, length us, event | category | flops | bytes accessed | tf_op | source)
XLA Modules:
  0.0 150.3 jit_solution(3680900816322471613)
XLA Ops:
  1.4 14.8 %all-to-all-start = ((bf16[16,8,768]{2,1,0:T(8,128)(2,1)}), bf16[16,8,768]{2,1,0:T(8,128)(2,1)S(1)}, u32[]{:S(2)}, u32[]{:S(2)}) async-start(bf16[16,8,768]{2,1,0:T(8,128)(2,1)} %broadcast_in_dim.74), calls=%async_computation | async-start | bytes 393216 | tf_op jit(solution)/shard_map/all_to_all | solution.py:31
  18.1 3.5 %collective-permute-start = (bf16[128,1024]{1,0:T(8,128)(2,1)S(1)}, bf16[128,1024]{1,0:T(8,128)(2,1)S(1)}, u32[]{:S(2)}, u32[]{:S(2)}) collective-permute-start(bf16[128,1024]{1,0:T(8,128)(2,1)S(1)} %get-tuple-element.20), channel_id=1, source_target_pairs={{0,128},{128,256},{256,384},{384,0},{1,129},{129,257},{257,385},{3... | collective-permute-start | bytes 786440 | tf_op jit(solution)/shard_map/ppermute | solution.py:223
  21.6 4.8 %collective-permute-start.1 = (bf16[128,1024]{1,0:T(8,128)(2,1)S(1)}, bf16[128,1024]{1,0:T(8,128)(2,1)S(1)}, u32[]{:S(2)}, u32[]{:S(2)}) collective-permute-start(bf16[128,1024]{1,0:T(8,128)(2,1)S(1)} %get-tuple-element.22), channel_id=1, source_target_pairs={{0,256},{128,384},{256,0},{384,128},{1,257},{129,385},{257,1},{385... | collective-permute-start | bytes 786440 | tf_op jit(solution)/shard_map/ppermute | solution.py:223
  26.4 3.3 %collective-permute-start.2 = (bf16[128,1024]{1,0:T(8,128)(2,1)S(1)}, bf16[128,1024]{1,0:T(8,128)(2,1)S(1)}, u32[]{:S(2)}, u32[]{:S(2)}) collective-permute-start(bf16[128,1024]{1,0:T(8,128)(2,1)S(1)} %get-tuple-element.19), channel_id=1, source_target_pairs={{0,384},{128,0},{256,128},{384,256},{1,385},{129,1},{257,129},{385... | collective-permute-start | bytes 786440 | tf_op jit(solution)/shard_map/ppermute | solution.py:223
  29.7 5.9 %collective-permute-done.1.rows2 = bf16[128,1024]{1,0:T(8,128)(2,1)S(1)} collective-permute-done((bf16[128,1024]{1,0:T(8,128)(2,1)S(1)}, bf16[128,1024]{1,0:T(8,128)(2,1)S(1)}, u32[]{:S(2)}, u32[]{:S(2)}) %collective-permute-start.1) | collective-permute-done | bytes 262176 | tf_op jit(solution)/shard_map/ppermute | solution.py:223
  37.9 4.3 %all-to-all-start.1 = ((bf16[4,16,8,768]{3,2,1,0:T(8,128)(2,1)}), bf16[4,16,8,768]{3,2,1,0:T(8,128)(2,1)S(1)}, u32[]{:S(2)}, u32[]{:S(2)}) async-start(bf16[4,16,8,768]{3,2,1,0:T(8,128)(2,1)} %broadcast_in_dim.75), calls=%async_computation.1 | async-start | bytes 1572864 | tf_op jit(solution)/shard_map/all_to_all | solution.py:31
  43.3 9.8 %all-to-all-done.1 = bf16[4,16,8,768]{3,2,1,0:T(8,128)(2,1)S(1)} async-done(((bf16[4,16,8,768]{3,2,1,0:T(8,128)(2,1)}), bf16[4,16,8,768]{3,2,1,0:T(8,128)(2,1)S(1)}, u32[]{:S(2)}, u32[]{:S(2)}) %all-to-all-start.1) | async-done | bytes 786464 | tf_op jit(solution)/shard_map/all_to_all | solution.py:31
  58.2 3.0 %project.2 = f32[4,128,256]{2,1,0:T(8,128)} custom-call(s32[2]{0:T(128)} %pad_add_fusion.2.where, bf16[128,1024]{1,0:T(8,128)(2,1)} %get-tuple-element.21.rows0, bf16[128,1024]{1,0:T(8,128)(2,1)} %copy-done.7, bf16[128,1024]{1,0:T(8,128)(2,1)} %copy-done.8, bf16[128,1024]{1,0:T(8,128)(2,1)} %copy-done.9, bf16[4,128,768]{2,1,0:T(8,128)(2,1)} %bitcast.20, ...), custom_call_target="tpu_custom_call" | custom-call | tf_op jit(solution)/shard_map/project/pallas_call | solution.py:255
  61.3 5.3 %all-to-all-start.2 = ((f32[4,128,256]{2,1,0:T(8,128)}), f32[4,128,256]{2,1,0:T(8,128)S(1)}, u32[]{:S(2)}, u32[]{:S(2)}) async-start(f32[4,128,256]{2,1,0:T(8,128)} %project.2), calls=%async_computation.2 | async-start | bytes 1048576 | tf_op jit(solution)/shard_map/all_to_all | solution.py:267
  67.3 3.6 %project.3 = f32[4,128,512]{2,1,0:T(8,128)} custom-call(s32[2]{0:T(128)} %pad_add_fusion.2.where, bf16[128,1024]{1,0:T(8,128)(2,1)} %get-tuple-element.21.rows0, bf16[128,1024]{1,0:T(8,128)(2,1)} %copy-done.7, bf16[128,1024]{1,0:T(8,128)(2,1)} %copy-done.8, bf16[128,1024]{1,0:T(8,128)(2,1)} %copy-done.9, bf16[4,128,768]{2,1,0:T(8,128)(2,1)} %bitcast.21, ...), custom_call_target="tpu_custom_call" | custom-call | tf_op jit(solution)/shard_map/project/pallas_call | solution.py:255
  70.9 5.4 %all-to-all-done.2.parts = f32[4,128,256]{2,1,0:T(8,128)S(1)} async-done(((f32[4,128,256]{2,1,0:T(8,128)}), f32[4,128,256]{2,1,0:T(8,128)S(1)}, u32[]{:S(2)}, u32[]{:S(2)}) %all-to-all-start.2) | async-done | bytes 524320 | tf_op jit(solution)/shard_map/all_to_all | solution.py:267
  78.9 7.4 %collective-permute-start.4 = (bf16[128,256]{1,0:T(8,128)(2,1)}, bf16[128,256]{1,0:T(8,128)(2,1)S(1)}, u32[]{:S(2)}, u32[]{:S(2)}) collective-permute-start(bf16[128,256]{1,0:T(8,128)(2,1)} %key_value.1), channel_id=1, source_target_pairs={{0,64},{16,80},{32,96},{48,112},{64,0},{80,16},{96,32},{112,48},{1... | collective-permute-start | bytes 196616 | tf_op jit(solution)/shard_map/ppermute | solution.py:26
  86.3 3.5 %all-to-all-start.3 = ((f32[4,128,512]{2,1,0:T(8,128)}), f32[4,128,512]{2,1,0:T(8,128)S(1)}, u32[]{:S(2)}, u32[]{:S(2)}) async-start(f32[4,128,512]{2,1,0:T(8,128)} %project.3), calls=%async_computation.3 | async-start | bytes 2097152 | tf_op jit(solution)/shard_map/all_to_all | solution.py:275
  90.0 5.1 %collective-permute-start.5 = (bf16[256,256]{1,0:T(8,128)(2,1)S(1)}, bf16[256,256]{1,0:T(8,128)(2,1)S(1)}, u32[]{:S(2)}, u32[]{:S(2)}) collective-permute-start(bf16[256,256]{1,0:T(8,128)(2,1)S(1)} %pad_maximum_fusion.1), channel_id=1, source_target_pairs={{0,32},{16,48},{32,0},{48,16},{64,96},{80,112},{96,64},{112,80},{1... | collective-permute-start | bytes 393224 | tf_op jit(solution)/shard_map/ppermute | solution.py:26
  95.1 3.5 %collective-permute-done.5 = bf16[256,256]{1,0:T(8,128)(2,1)S(1)} collective-permute-done((bf16[256,256]{1,0:T(8,128)(2,1)S(1)}, bf16[256,256]{1,0:T(8,128)(2,1)S(1)}, u32[]{:S(2)}, u32[]{:S(2)}) %collective-permute-start.5) | collective-permute-done | bytes 131104 | tf_op jit(solution)/shard_map/ppermute | solution.py:26
  98.6 5.6 %collective-permute-start.6 = (bf16[512,256]{1,0:T(8,128)(2,1)S(1)}, bf16[512,256]{1,0:T(8,128)(2,1)S(1)}, u32[]{:S(2)}, u32[]{:S(2)}) collective-permute-start(bf16[512,256]{1,0:T(8,128)(2,1)S(1)} %pad_maximum_fusion.own_near), channel_id=1, source_target_pairs={{0,16},{16,0},{32,48},{48,32},{64,80},{80,64},{96,112},{112,96},{1... | collective-permute-start | bytes 786440 | tf_op jit(solution)/shard_map/ppermute | solution.py:26
  109.8 4.0 %all-to-all-start.4 = ((bf16[4,512,128]{2,1,0:T(8,128)(2,1)}), bf16[4,512,128]{2,1,0:T(8,128)(2,1)S(1)}, u32[]{:S(2)}, u32[]{:S(2)}) async-start(bf16[4,512,128]{2,1,0:T(8,128)(2,1)} %query.1), calls=%async_computation.4 | async-start | bytes 1048576 | tf_op jit(solution)/shard_map/all_to_all | solution.py:291
  115.8 2.4 %collective-permute-start.8 = (bf16[512,256]{1,0:T(8,128)(2,1)S(1)}, bf16[512,256]{1,0:T(8,128)(2,1)S(1)}, u32[]{:S(2)}, u32[]{:S(2)}) collective-permute-start(bf16[512,256]{1,0:T(8,128)(2,1)S(1)} %collective-permute-done.6.own_far), channel_id=1, source_target_pairs={{0,8},{8,0},{1,9},{9,1},{2,10},{10,2},{3,11},{11,3},{4,12},{12,4},... | collective-permute-start | bytes 786440 | tf_op jit(solution)/shard_map/ppermute | solution.py:26
  120.6 2.6 %order.1 = (bf16[2048,128]{1,0:T(8,128)(2,1)}, bf16[2048,256]{1,0:T(8,128)(2,1)}) custom-call(s32[45]{0:T(128)} %pad_add_fusion.1.plan, bf16[512,256]{1,0:T(8,128)(2,1)} %copy-done.6, bf16[512,256]{1,0:T(8,128)(2,1)} %copy-done.11, bf16[512,256]{1,0:T(8,128)(2,1)} %copy-done.12, bf16[512,256]{1,0:T(8,128)(2,1)} %copy-done.13), custom_call_target="tpu_custom_call" | custom-call | tf_op jit(solution)/shard_map/order/pallas_call | solution.py:293
  124.0 7.1 %peers.1 = bf16[4,128,640]{2,1,0:T(8,128)(2,1)} custom-call(s32[45]{0:T(128)} %pad_add_fusion.1.plan, bf16[4,512,128]{2,1,0:T(8,128)(2,1)} %copy-done.5, bf16[2048,128]{1,0:T(8,128)(2,1)} %get-tuple-element.14.keys, bf16[2048,256]{1,0:T(8,128)(2,1)} %get-tuple-element.15.values), custom_call_target="tpu_custom_call" | custom-call | tf_op jit(solution)/shard_map/peers/pallas_call | solution.py:304
  131.1 4.8 %all-to-all-start.5 = ((bf16[4,128,640]{2,1,0:T(8,128)(2,1)}), bf16[4,128,640]{2,1,0:T(8,128)(2,1)S(1)}, u32[]{:S(2)}, u32[]{:S(2)}) async-start(bf16[4,128,640]{2,1,0:T(8,128)(2,1)} %peers.1), calls=%async_computation.5 | async-start | bytes 1310720 | tf_op jit(solution)/shard_map/all_to_all | solution.py:320
  135.9 3.8 %own.1 = bf16[128,640]{1,0:T(8,128)(2,1)} custom-call(s32[45]{0:T(128)} %pad_add_fusion.1.plan, bf16[4,512,128]{2,1,0:T(8,128)(2,1)} %query.1, bf16[2048,128]{1,0:T(8,128)(2,1)} %get-tuple-element.14.keys, bf16[2048,256]{1,0:T(8,128)(2,1)} %get-tuple-element.15.values), custom_call_target="tpu_custom_call" | custom-call | tf_op jit(solution)/shard_map/own/pallas_call | solution.py:312
  139.7 7.3 %all-to-all-done.5.parts = bf16[4,128,640]{2,1,0:T(8,128)(2,1)S(1)} async-done(((bf16[4,128,640]{2,1,0:T(8,128)(2,1)}), bf16[4,128,640]{2,1,0:T(8,128)(2,1)S(1)}, u32[]{:S(2)}, u32[]{:S(2)}) %all-to-all-start.5) | async-done | bytes 655392 | tf_op jit(solution)/shard_map/all_to_all | solution.py:320
  147.8 2.5 %combine.1 = bf16[128,512]{1,0:T(8,128)(2,1)} custom-call(s32[45]{0:T(128)} %pad_add_fusion.1.plan, bf16[4,128,640]{2,1,0:T(8,128)(2,1)} %copy-done.3, bf16[128,640]{1,0:T(8,128)(2,1)} %own.1), custom_call_target="tpu_custom_call" | custom-call | tf_op jit(solution)/shard_map/combine/pallas_call | solution.py:321
  (75 shorter events, 25.8 us)
Async XLA Ops:
  1.4 35.5 %all-to-all-start = ((bf16[16,8,768]{2,1,0:T(8,128)(2,1)}), bf16[16,8,768]{2,1,0:T(8,128)(2,1)S(1)}, u32[]{:S(2)}, u32[]{:S(2)}) async-start(bf16[16,8,768]{2,1,0:T(8,128)(2,1)} %broadcast_in_dim.74), calls=%async_computation | async-start | bytes 393216 | tf_op jit(solution)/shard_map/all_to_all | solution.py:31
  18.1 11.6 %collective-permute-start = (bf16[128,1024]{1,0:T(8,128)(2,1)S(1)}, bf16[128,1024]{1,0:T(8,128)(2,1)S(1)}, u32[]{:S(2)}, u32[]{:S(2)}) collective-permute-start(bf16[128,1024]{1,0:T(8,128)(2,1)S(1)} %get-tuple-element.20), channel_id=1, source_target_pairs={{0,128},{128,256},{256,384},{384,0},{1,129},{129,257},{257,385},{3... | collective-permute-start | bytes 786440 | tf_op jit(solution)/shard_map/ppermute | solution.py:223
  21.6 14.0 %collective-permute-start.1 = (bf16[128,1024]{1,0:T(8,128)(2,1)S(1)}, bf16[128,1024]{1,0:T(8,128)(2,1)S(1)}, u32[]{:S(2)}, u32[]{:S(2)}) collective-permute-start(bf16[128,1024]{1,0:T(8,128)(2,1)S(1)} %get-tuple-element.22), channel_id=1, source_target_pairs={{0,256},{128,384},{256,0},{384,128},{1,257},{129,385},{257,1},{385... | collective-permute-start | bytes 786440 | tf_op jit(solution)/shard_map/ppermute | solution.py:223
  26.4 10.5 %collective-permute-start.2 = (bf16[128,1024]{1,0:T(8,128)(2,1)S(1)}, bf16[128,1024]{1,0:T(8,128)(2,1)S(1)}, u32[]{:S(2)}, u32[]{:S(2)}) collective-permute-start(bf16[128,1024]{1,0:T(8,128)(2,1)S(1)} %get-tuple-element.19), channel_id=1, source_target_pairs={{0,384},{128,0},{256,128},{384,256},{1,385},{129,1},{257,129},{385... | collective-permute-start | bytes 786440 | tf_op jit(solution)/shard_map/ppermute | solution.py:223
  29.7 8.1 %copy-start.7 = (bf16[128,1024]{1,0:T(8,128)(2,1)}, bf16[128,1024]{1,0:T(8,128)(2,1)S(1)}, u32[]{:S(2)}) copy-start(bf16[128,1024]{1,0:T(8,128)(2,1)S(1)} %collective-permute-done.rows1) | copy-start | bytes 786436
  35.6 2.3 %copy-start.8 = (bf16[128,1024]{1,0:T(8,128)(2,1)}, bf16[128,1024]{1,0:T(8,128)(2,1)S(1)}, u32[]{:S(2)}) copy-start(bf16[128,1024]{1,0:T(8,128)(2,1)S(1)} %collective-permute-done.1.rows2) | copy-start | bytes 786436
  36.9 1.0 copy-start.9
  37.9 15.3 %all-to-all-start.1 = ((bf16[4,16,8,768]{3,2,1,0:T(8,128)(2,1)}), bf16[4,16,8,768]{3,2,1,0:T(8,128)(2,1)S(1)}, u32[]{:S(2)}, u32[]{:S(2)}) async-start(bf16[4,16,8,768]{3,2,1,0:T(8,128)(2,1)} %broadcast_in_dim.75), calls=%async_computation.1 | async-start | bytes 1572864 | tf_op jit(solution)/shard_map/all_to_all | solution.py:31
  53.1 4.2 %copy-start = (bf16[4,16,8,768]{3,2,1,0:T(8,128)(2,1)}, bf16[4,16,8,768]{3,2,1,0:T(8,128)(2,1)S(1)}, u32[]{:S(2)}) copy-start(bf16[4,16,8,768]{3,2,1,0:T(8,128)(2,1)S(1)} %all-to-all-done.1) | copy-start | bytes 2359300
  53.1 4.2 %collective-permute-start.3 = (bf16[4,128,768]{2,1,0:T(8,128)(2,1)S(1)}, bf16[4,128,768]{2,1,0:T(8,128)(2,1)S(1)}, u32[]{:S(2)}, u32[]{:S(2)}) collective-permute-start(bf16[4,128,768]{2,1,0:T(8,128)(2,1)S(1)} %bitcast.19), channel_id=1, source_target_pairs={{0,8},{8,0},{1,9},{9,1},{2,10},{10,2},{3,11},{11,3},{4,12},{12,4},... | collective-permute-start | bytes 2359304 | tf_op jit(solution)/shard_map/ppermute | solution.py:26
  57.3 0.9 copy-start.2
  61.3 15.0 %all-to-all-start.2 = ((f32[4,128,256]{2,1,0:T(8,128)}), f32[4,128,256]{2,1,0:T(8,128)S(1)}, u32[]{:S(2)}, u32[]{:S(2)}) async-start(f32[4,128,256]{2,1,0:T(8,128)} %project.2), calls=%async_computation.2 | async-start | bytes 1048576 | tf_op jit(solution)/shard_map/all_to_all | solution.py:267
  78.9 11.1 %copy-start.10 = (bf16[128,256]{1,0:T(8,128)(2,1)S(1)}, bf16[128,256]{1,0:T(8,128)(2,1)}, u32[]{:S(2)}) copy-start(bf16[128,256]{1,0:T(8,128)(2,1)} %key_value.1) | copy-start | bytes 196612
  78.9 11.1 %collective-permute-start.4 = (bf16[128,256]{1,0:T(8,128)(2,1)}, bf16[128,256]{1,0:T(8,128)(2,1)S(1)}, u32[]{:S(2)}, u32[]{:S(2)}) collective-permute-start(bf16[128,256]{1,0:T(8,128)(2,1)} %key_value.1), channel_id=1, source_target_pairs={{0,64},{16,80},{32,96},{48,112},{64,0},{80,16},{96,32},{112,48},{1... | collective-permute-start | bytes 196616 | tf_op jit(solution)/shard_map/ppermute | solution.py:26
  86.3 20.3 %all-to-all-start.3 = ((f32[4,128,512]{2,1,0:T(8,128)}), f32[4,128,512]{2,1,0:T(8,128)S(1)}, u32[]{:S(2)}, u32[]{:S(2)}) async-start(f32[4,128,512]{2,1,0:T(8,128)} %project.3), calls=%async_computation.3 | async-start | bytes 2097152 | tf_op jit(solution)/shard_map/all_to_all | solution.py:275
  90.0 8.6 %collective-permute-start.5 = (bf16[256,256]{1,0:T(8,128)(2,1)S(1)}, bf16[256,256]{1,0:T(8,128)(2,1)S(1)}, u32[]{:S(2)}, u32[]{:S(2)}) collective-permute-start(bf16[256,256]{1,0:T(8,128)(2,1)S(1)} %pad_maximum_fusion.1), channel_id=1, source_target_pairs={{0,32},{16,48},{32,0},{48,16},{64,96},{80,112},{96,64},{112,80},{1... | collective-permute-start | bytes 393224 | tf_op jit(solution)/shard_map/ppermute | solution.py:26
  98.6 15.2 %copy-start.6 = (bf16[512,256]{1,0:T(8,128)(2,1)}, bf16[512,256]{1,0:T(8,128)(2,1)S(1)}, u32[]{:S(2)}) copy-start(bf16[512,256]{1,0:T(8,128)(2,1)S(1)} %pad_maximum_fusion.own_near) | copy-start | bytes 786436
  98.6 17.1 %collective-permute-start.6 = (bf16[512,256]{1,0:T(8,128)(2,1)S(1)}, bf16[512,256]{1,0:T(8,128)(2,1)S(1)}, u32[]{:S(2)}, u32[]{:S(2)}) collective-permute-start(bf16[512,256]{1,0:T(8,128)(2,1)S(1)} %pad_maximum_fusion.own_near), channel_id=1, source_target_pairs={{0,16},{16,0},{32,48},{48,32},{64,80},{80,64},{96,112},{112,96},{1... | collective-permute-start | bytes 786440 | tf_op jit(solution)/shard_map/ppermute | solution.py:26
  106.6 1.0 copy-start.1
  109.8 13.4 %all-to-all-start.4 = ((bf16[4,512,128]{2,1,0:T(8,128)(2,1)}), bf16[4,512,128]{2,1,0:T(8,128)(2,1)S(1)}, u32[]{:S(2)}, u32[]{:S(2)}) async-start(bf16[4,512,128]{2,1,0:T(8,128)(2,1)} %query.1), calls=%async_computation.4 | async-start | bytes 1048576 | tf_op jit(solution)/shard_map/all_to_all | solution.py:291
  113.8 5.3 %collective-permute-start.7 = (bf16[512,256]{1,0:T(8,128)(2,1)S(1)}, bf16[512,256]{1,0:T(8,128)(2,1)S(1)}, u32[]{:S(2)}, u32[]{:S(2)}) collective-permute-start(bf16[512,256]{1,0:T(8,128)(2,1)S(1)} %pad_maximum_fusion.own_near), channel_id=1, source_target_pairs={{0,8},{8,0},{1,9},{9,1},{2,10},{10,2},{3,11},{11,3},{4,12},{12,4},... | collective-permute-start | bytes 786440 | tf_op jit(solution)/shard_map/ppermute | solution.py:26
  115.8 3.6 %copy-start.11 = (bf16[512,256]{1,0:T(8,128)(2,1)}, bf16[512,256]{1,0:T(8,128)(2,1)S(1)}, u32[]{:S(2)}) copy-start(bf16[512,256]{1,0:T(8,128)(2,1)S(1)} %collective-permute-done.6.own_far) | copy-start | bytes 786436
  115.8 3.6 %collective-permute-start.8 = (bf16[512,256]{1,0:T(8,128)(2,1)S(1)}, bf16[512,256]{1,0:T(8,128)(2,1)S(1)}, u32[]{:S(2)}, u32[]{:S(2)}) collective-permute-start(bf16[512,256]{1,0:T(8,128)(2,1)S(1)} %collective-permute-done.6.own_far), channel_id=1, source_target_pairs={{0,8},{8,0},{1,9},{9,1},{2,10},{10,2},{3,11},{11,3},{4,12},{12,4},... | collective-permute-start | bytes 786440 | tf_op jit(solution)/shard_map/ppermute | solution.py:26
  131.1 15.9 %all-to-all-start.5 = ((bf16[4,128,640]{2,1,0:T(8,128)(2,1)}), bf16[4,128,640]{2,1,0:T(8,128)(2,1)S(1)}, u32[]{:S(2)}, u32[]{:S(2)}) async-start(bf16[4,128,640]{2,1,0:T(8,128)(2,1)} %peers.1), calls=%async_computation.5 | async-start | bytes 1310720 | tf_op jit(solution)/shard_map/all_to_all | solution.py:320
  (6 other events, 4.6 us)

commit v3 on v2

--- a/solution.py
+++ b/solution.py
@@ -43,8 +43,23 @@
     )
 
 
-def key_value_kernel(parts, cosine, sine, out):
-    total = parts[0] + parts[1] + parts[2] + parts[3]
+def gather_rows(weight, source, outer, base, first, width):
+    for block in range(outer):
+        for group in range(8):
+            for half in range(2):
+                rows = [
+                    source[block * 4 + x, (group * 2 + half) * 8 : (group * 2 + half) * 8 + 8, first : first + width]
+                    for x in range(4)
+                ]
+                target = pl.multiple_of(block * 1024 + group * 128 + half * 32 + base, 32)
+                weight[pl.ds(target, 32), :] = jnp.concatenate(rows, axis=0)
+
+
+def key_value_kernel(where, rows, mine, across, cosine, sine, out, weight):
+    core = where[1]
+    for far, source in enumerate((mine, across)):
+        gather_rows(weight, source, 4, (core ^ far) * 64, 0, 2 * HEAD)
+    total = jnp.dot(rows[...], weight[...], preferred_element_type=jnp.float32)
     key = total[:, :HEAD]
     turned = key * cosine[...] + pltpu.roll(key, HEAD // 2, 1) * sine[...]
     out[:, :HEAD] = turned.astype(jnp.bfloat16)
@@ -68,18 +83,8 @@
 def project_kernel(where, rows0, rows1, rows2, rows3, mine, across, out, weight):
     y = where[0]
     core = where[1]
-    width = out.shape[2]
-    first = 0 if width == 2 * HEAD else 2 * HEAD
     for far, source in enumerate((mine, across)):
-        base = (core ^ far) * 64
-        for group in range(8):
-            for half in range(2):
-                rows = [
-                    source[x, (group * 2 + half) * 8 : (group * 2 + half) * 8 + 8, first : first + width]
-                    for x in range(4)
-                ]
-                target = pl.multiple_of(group * 128 + half * 32 + base, 32)
-                weight[pl.ds(target, 32), :] = jnp.concatenate(rows, axis=0)
+        gather_rows(weight, source, 1, (core ^ far) * 64, 0, HEADS * HEAD)
     for shift, rows in enumerate((rows0, rows1, rows2, rows3)):
         out[(y + 4 - shift) % 4] = jnp.dot(
             rows[...], weight[...], preferred_element_type=jnp.float32
@@ -203,6 +208,13 @@
         out[:, head * HEAD : (head + 1) * HEAD] = (mixed / whole).astype(jnp.bfloat16)
 
 
+def in_vmem(*values):
+    return tuple(pltpu.with_memory_space_constraint(value, pltpu.VMEM) for value in values)
+
+
+limits = pltpu.CompilerParams(vmem_limit_bytes=16 * 1024 * 1024)
+
+
 def after(value, *others):
     return lax.optimization_barrier((value,) + others)[0]
 
@@ -222,9 +234,14 @@
         if shift:
             piece = lax.ppermute(piece, "y", [(i, (i + shift) % 4) for i in range(4)])
         sliced.append(piece)
-    along_z = after(along_z, *sliced)
-    along_x = spread(along_z, "x", 4).reshape(4, ROWS, 768)
-    across = swap(along_x, "core", 2, 1)
+    along_z = after(along_z, sliced[1])
+    narrow = spread(along_z[:, :, : 2 * HEAD], "x", 4)
+    narrow = after(narrow, sliced[3])
+    narrow = spread(narrow, "y", 4).reshape(16, ROWS, 2 * HEAD)
+    narrow = after(narrow, sliced[2])
+    narrow_across = swap(narrow, "core", 2, 1)
+    wide, _ = lax.optimization_barrier((along_z[:, :, 2 * HEAD :], narrow))
+    wide = spread(wide, "x", 4).reshape(4, ROWS, HEADS * HEAD)
 
     table = stretch_table.reshape(4, 8, 2, 2)
     own_stretches = table[y, zl, core]
@@ -251,28 +268,27 @@
     where = jnp.stack([y, core]).astype(jnp.int32)
     flip = (own_stretches[:1] > own_stretches[1:]).astype(jnp.int32)
 
-    def project(width, across):
-        part = pl.pallas_call(
-            project_kernel,
-            out_shape=jax.ShapeDtypeStruct((4, ROWS, width), f32),
-            in_specs=[smem] + [vmem] * 6,
-            out_specs=vmem,
-            scratch_shapes=[pltpu.VMEM((1024, width), bf16)],
-            name="project",
-        )(where, *sliced, along_x, across)
-        return part
-
-    part = project(2 * HEAD, across)
-    query_part = project(HEADS * HEAD, after(across, part))
-    part = lax.all_to_all(part, "y", 0, 0)
     key_value = pl.pallas_call(
         key_value_kernel,
-        out_shape=jax.ShapeDtypeStruct((ROWS, 2 * HEAD), bf16),
-        in_specs=[vmem] * 3,
-        out_specs=vmem,
+        out_shape=pltpu.VMEM((ROWS, 2 * HEAD), bf16),
+        in_specs=[smem] + [vmem] * 5,
+        out_specs=vmem,
+        scratch_shapes=[pltpu.VMEM((4096, 2 * HEAD), bf16)],
+        compiler_params=limits,
         name="key_value",
-    )(part, cosine, sine)
-    query_part = lax.all_to_all(after(query_part, key_value), "y", 0, 0)
+    )(where, *in_vmem(rows, narrow, narrow_across, cosine, sine))
+    wide = after(wide, key_value)
+    wide_across = swap(wide, "core", 2, 1)
+    query_part = pl.pallas_call(
+        project_kernel,
+        out_shape=pltpu.VMEM((4, ROWS, HEADS * HEAD), f32),
+        in_specs=[smem] + [vmem] * 6,
+        out_specs=vmem,
+        scratch_shapes=[pltpu.VMEM((1024, HEADS * HEAD), bf16)],
+        compiler_params=limits,
+        name="project",
+    )(where, *in_vmem(*sliced, wide, wide_across))
+    query_part = lax.all_to_all(query_part, "y", 0, 0)
 
     step = swap(key_value, "zl", 8, 4)
     step = jnp.concatenate([key_value, step], axis=0)
@@ -283,48 +299,53 @@
 
     query = pl.pallas_call(
         query_kernel,
-        out_shape=jax.ShapeDtypeStruct((4, HEADS * ROWS, HEAD), bf16),
+        out_shape=pltpu.VMEM((4, HEADS * ROWS, HEAD), bf16),
         in_specs=[smem] + [vmem] * 3,
         out_specs=vmem,
+        compiler_params=limits,
         name="query",
-    )(flip, query_part, cosine, sine)
+    )(flip, *in_vmem(query_part, cosine, sine))
     queries = lax.all_to_all(query, "y", 0, 0)
 
     keys, values = pl.pallas_call(
         order_kernel,
         out_shape=(
-            jax.ShapeDtypeStruct((KEYS, HEAD), bf16),
-            jax.ShapeDtypeStruct((KEYS, 2 * HEAD), bf16),
+            pltpu.VMEM((KEYS, HEAD), bf16),
+            pltpu.VMEM((KEYS, 2 * HEAD), bf16),
         ),
         in_specs=[smem] + [vmem] * 4,
         out_specs=(vmem, vmem),
+        compiler_params=limits,
         name="order",
-    )(plan, near, far, other_near, other_far)
+    )(plan, *in_vmem(near, far, other_near, other_far))
     score_scratch = [pltpu.VMEM((6, HEADS * STRETCH, CHUNK), f32)]
     partial = pl.pallas_call(
         peers_kernel,
-        out_shape=jax.ShapeDtypeStruct((4, ROWS, HEADS * HEAD + HEAD), bf16),
+        out_shape=pltpu.VMEM((4, ROWS, HEADS * HEAD + HEAD), bf16),
         in_specs=[smem] + [vmem] * 3,
         out_specs=vmem,
         scratch_shapes=score_scratch,
+        compiler_params=limits,
         name="peers",
-    )(plan, queries, keys, values)
+    )(plan, *in_vmem(queries, keys, values))
     own_partial = pl.pallas_call(
         own_kernel,
-        out_shape=jax.ShapeDtypeStruct((ROWS, HEADS * HEAD + HEAD), bf16),
+        out_shape=pltpu.VMEM((ROWS, HEADS * HEAD + HEAD), bf16),
         in_specs=[smem] + [vmem] * 3,
         out_specs=vmem,
         scratch_shapes=score_scratch,
+        compiler_params=limits,
         name="own",
-    )(plan, after(query, partial), keys, values)
+    )(plan, *in_vmem(after(query, partial), keys, values))
     partial = lax.all_to_all(partial, "y", 0, 0)
     attended = pl.pallas_call(
         combine_kernel,
         out_shape=jax.ShapeDtypeStruct((ROWS, HEADS * HEAD), bf16),
         in_specs=[smem] + [vmem] * 2,
         out_specs=vmem,
+        compiler_params=limits,
         name="combine",
-    )(plan, partial, own_partial)
+    )(plan, *in_vmem(partial, own_partial))
     return attended[None]
 
 

time: 151 us -> 153 us (1.013)
  the two profiles are of different devices: /device:TPU:64 before, /device:TPU:32 now
where the time goes in v3:
time: 153 us; the launch traced here: 152 us
  starting transfers between devices  70.3 us (46%)
  waiting for transfers between devices  52.1 us (34%)
  Pallas kernels  17 us (11%)
  local copies, waits for them, and re-layouts  8.39 us (5%)
  other arithmetic  2.42 us (2%)
  between operations  1.58 us (1%)
    all_to_all x4, starting transfers between devices, spread(): return lax.all_to_all(copies, axis, 0, 0)  27.4 us
    all_to_all x4, waiting for transfers between devices, spread(): return lax.all_to_all(copies, axis, 0, 0)  20.5 us
    ppermute x7, starting transfers between devices, swap(): return lax.ppermute(value, axis, [(i, i ^ distance) for i in range(size)])  19.9 us
    ppermute x3, starting transfers between devices, on_device(): piece = lax.ppermute(piece, 'y', [(i, (i + shift) % 4) for i in range(4)])  12.5 us
    ppermute x3, waiting for transfers between devices, on_device(): piece = lax.ppermute(piece, 'y', [(i, (i + shift) % 4) for i in range(4)])  11.9 us
    all_to_all x1, waiting for transfers between devices, on_device(): partial = lax.all_to_all(partial, 'y', 0, 0)  7.05 us
    ppermute x7, waiting for transfers between devices, swap(): return lax.ppermute(value, axis, [(i, i ^ distance) for i in range(size)])  6.86 us
    pallas_call x1, Pallas kernels, on_device(): pl.pallas_call(peers_kernel, out_shape=pltpu.VMEM((4, ROWS, HEADS * HEAD...  6.24 us
  transfers between devices with their start and end apart: 17, of which 10 were waited for; matrix products, arithmetic and copies ran while one was open for 4% of the time, Pallas kernels for 6%

profile of v3, /device:TPU:32, one launch (start us, length us, event | category | flops | bytes accessed | tf_op | source)
XLA Modules:
  0.0 151.8 jit_solution(16777905816994896403)
XLA Ops:
  1.4 15.2 %all-to-all-start = ((bf16[16,8,768]{2,1,0:T(8,128)(2,1)}), bf16[16,8,768]{2,1,0:T(8,128)(2,1)S(1)}, u32[]{:S(2)}, u32[]{:S(2)}) async-start(bf16[16,8,768]{2,1,0:T(8,128)(2,1)} %broadcast_in_dim.86), calls=%async_computation | async-start | bytes 393216 | tf_op jit(solution)/shard_map/all_to_all | solution.py:31
  17.9 3.5 %collective-permute-start = (bf16[128,1024]{1,0:T(8,128)(2,1)S(1)}, bf16[128,1024]{1,0:T(8,128)(2,1)S(1)}, u32[]{:S(2)}, u32[]{:S(2)}) collective-permute-start(bf16[128,1024]{1,0:T(8,128)(2,1)S(1)} %get-tuple-element.25), channel_id=1, source_target_pairs={{0,128},{128,256},{256,384},{384,0},{1,129},{129,257},{257,385},{3... | collective-permute-start | bytes 786440 | tf_op jit(solution)/shard_map/ppermute | solution.py:235
  21.4 3.6 %collective-permute-start.2 = (bf16[128,1024]{1,0:T(8,128)(2,1)S(1)}, bf16[128,1024]{1,0:T(8,128)(2,1)S(1)}, u32[]{:S(2)}, u32[]{:S(2)}) collective-permute-start(bf16[128,1024]{1,0:T(8,128)(2,1)S(1)} %get-tuple-element.23), channel_id=1, source_target_pairs={{0,384},{128,0},{256,128},{384,256},{1,385},{129,1},{257,129},{385... | collective-permute-start | bytes 786440 | tf_op jit(solution)/shard_map/ppermute | solution.py:235
  25.0 3.6 %collective-permute-done.rows1 = bf16[128,1024]{1,0:T(8,128)(2,1)S(1)} collective-permute-done((bf16[128,1024]{1,0:T(8,128)(2,1)S(1)}, bf16[128,1024]{1,0:T(8,128)(2,1)S(1)}, u32[]{:S(2)}, u32[]{:S(2)}) %collective-permute-start) | collective-permute-done | bytes 262176 | tf_op jit(solution)/shard_map/ppermute | solution.py:235
  28.5 6.1 %all-to-all-done = bf16[16,8,768]{2,1,0:T(8,128)(2,1)S(1)} async-done(((bf16[16,8,768]{2,1,0:T(8,128)(2,1)}), bf16[16,8,768]{2,1,0:T(8,128)(2,1)S(1)}, u32[]{:S(2)}, u32[]{:S(2)}) %all-to-all-start) | async-done | bytes 196640 | tf_op jit(solution)/shard_map/all_to_all | solution.py:31
  35.4 4.3 %all-to-all-start.1 = ((bf16[4,16,8,256]{3,2,1,0:T(8,128)(2,1)}), bf16[4,16,8,256]{3,2,1,0:T(8,128)(2,1)S(1)}, u32[]{:S(2)}, u32[]{:S(2)}) async-start(bf16[4,16,8,256]{3,2,1,0:T(8,128)(2,1)} %broadcast_in_dim.87), calls=%async_computation.1 | async-start | bytes 524288 | tf_op jit(solution)/shard_map/all_to_all | solution.py:31
  39.7 6.7 %all-to-all-done.1 = bf16[4,16,8,256]{3,2,1,0:T(8,128)(2,1)S(1)} async-done(((bf16[4,16,8,256]{3,2,1,0:T(8,128)(2,1)}), bf16[4,16,8,256]{3,2,1,0:T(8,128)(2,1)S(1)}, u32[]{:S(2)}, u32[]{:S(2)}) %all-to-all-start.1) | async-done | bytes 262176 | tf_op jit(solution)/shard_map/all_to_all | solution.py:31
  47.4 4.5 %all-to-all-start.2 = ((bf16[4,4,16,8,256]{4,3,2,1,0:T(8,128)(2,1)}), bf16[4,4,16,8,256]{4,3,2,1,0:T(8,128)(2,1)S(1)}, u32[]{:S(2)}, u32[]{:S(2)}) async-start(bf16[4,4,16,8,256]{4,3,2,1,0:T(8,128)(2,1)} %broadcast_in_dim.88), calls=%async_computation.2 | async-start | bytes 2097152 | tf_op jit(solution)/shard_map/all_to_all | solution.py:31
  51.9 5.4 %collective-permute-start.1 = (bf16[128,1024]{1,0:T(8,128)(2,1)S(1)}, bf16[128,1024]{1,0:T(8,128)(2,1)S(1)}, u32[]{:S(2)}, u32[]{:S(2)}) collective-permute-start(bf16[128,1024]{1,0:T(8,128)(2,1)S(1)} %get-tuple-element.24), channel_id=1, source_target_pairs={{0,256},{128,384},{256,0},{384,128},{1,257},{129,385},{257,1},{385... | collective-permute-start | bytes 786440 | tf_op jit(solution)/shard_map/ppermute | solution.py:235
  57.3 8.4 %collective-permute-done.1.rows2 = bf16[128,1024]{1,0:T(8,128)(2,1)S(1)} collective-permute-done((bf16[128,1024]{1,0:T(8,128)(2,1)S(1)}, bf16[128,1024]{1,0:T(8,128)(2,1)S(1)}, u32[]{:S(2)}, u32[]{:S(2)}) %collective-permute-start.1) | collective-permute-done | bytes 262176 | tf_op jit(solution)/shard_map/ppermute | solution.py:235
  69.6 3.5 %all-to-all-start.3 = ((bf16[4,16,8,512]{3,2,1,0:T(8,128)(2,1)}), bf16[4,16,8,512]{3,2,1,0:T(8,128)(2,1)S(1)}, u32[]{:S(2)}, u32[]{:S(2)}) async-start(bf16[4,16,8,512]{3,2,1,0:T(8,128)(2,1)} %broadcast_in_dim.89), calls=%async_computation.3 | async-start | bytes 1048576 | tf_op jit(solution)/shard_map/all_to_all | solution.py:31
  75.8 7.7 %all-to-all-done.3 = bf16[4,16,8,512]{3,2,1,0:T(8,128)(2,1)S(1)} async-done(((bf16[4,16,8,512]{3,2,1,0:T(8,128)(2,1)}), bf16[4,16,8,512]{3,2,1,0:T(8,128)(2,1)S(1)}, u32[]{:S(2)}, u32[]{:S(2)}) %all-to-all-start.3) | async-done | bytes 524320 | tf_op jit(solution)/shard_map/all_to_all | solution.py:31
  85.6 7.6 %collective-permute-start.5 = (bf16[128,256]{1,0:T(8,128)(2,1)S(1)}, bf16[128,256]{1,0:T(8,128)(2,1)S(1)}, u32[]{:S(2)}, u32[]{:S(2)}) collective-permute-start(bf16[128,256]{1,0:T(8,128)(2,1)S(1)} %key_value.1), channel_id=1, source_target_pairs={{0,64},{16,80},{32,96},{48,112},{64,0},{80,16},{96,32},{112,48},{1... | collective-permute-start | bytes 196616 | tf_op jit(solution)/shard_map/ppermute | solution.py:26
  95.1 2.4 %project.1 = f32[4,128,512]{2,1,0:T(8,128)} custom-call(s32[2]{0:T(128)S(1)} %pad_add_fusion.2.where, bf16[128,1024]{1,0:T(8,128)(2,1)S(1)} %get-tuple-element.26.rows0, bf16[128,1024]{1,0:T(8,128)(2,1)S(1)} %collective-permute-done.rows1, bf16[128,1024]{1,0:T(8,128)(2,1)S(1)} %copy-done.4, bf16[128,1024]{1,0:T(8,128)(2,1)S(1)} %copy-done.2, ...), custom_call_target="tpu_custom_call" | custom-call | tf_op jit(solution)/shard_map/project/pallas_call | solution.py:282
  97.5 3.5 %all-to-all-start.4 = ((f32[4,128,512]{2,1,0:T(8,128)}), f32[4,128,512]{2,1,0:T(8,128)S(1)}, u32[]{:S(2)}, u32[]{:S(2)}) async-start(f32[4,128,512]{2,1,0:T(8,128)} %project.1), calls=%async_computation.4 | async-start | bytes 2097152 | tf_op jit(solution)/shard_map/all_to_all | solution.py:291
  103.4 6.2 %collective-permute-done.6 = bf16[256,256]{1,0:T(8,128)(2,1)S(1)} collective-permute-done((bf16[256,256]{1,0:T(8,128)(2,1)S(1)}, bf16[256,256]{1,0:T(8,128)(2,1)S(1)}, u32[]{:S(2)}, u32[]{:S(2)}) %collective-permute-start.6) | collective-permute-done | bytes 131104 | tf_op jit(solution)/shard_map/ppermute | solution.py:26
  113.9 2.8 %all-to-all-done.4.parts = f32[4,128,512]{2,1,0:T(8,128)S(1)} async-done(((f32[4,128,512]{2,1,0:T(8,128)}), f32[4,128,512]{2,1,0:T(8,128)S(1)}, u32[]{:S(2)}, u32[]{:S(2)}) %all-to-all-start.4) | async-done | bytes 1048608 | tf_op jit(solution)/shard_map/all_to_all | solution.py:291
  117.7 3.5 %all-to-all-start.5 = ((bf16[4,512,128]{2,1,0:T(8,128)(2,1)}), bf16[4,512,128]{2,1,0:T(8,128)(2,1)S(1)}, u32[]{:S(2)}, u32[]{:S(2)}) async-start(bf16[4,512,128]{2,1,0:T(8,128)(2,1)} %query.1), calls=%async_computation.5 | async-start | bytes 1048576 | tf_op jit(solution)/shard_map/all_to_all | solution.py:308
  123.1 2.4 %collective-permute-start.9 = (bf16[512,256]{1,0:T(8,128)(2,1)S(1)}, bf16[512,256]{1,0:T(8,128)(2,1)S(1)}, u32[]{:S(2)}, u32[]{:S(2)}) collective-permute-start(bf16[512,256]{1,0:T(8,128)(2,1)S(1)} %collective-permute-done.7.own_far), channel_id=1, source_target_pairs={{0,8},{8,0},{1,9},{9,1},{2,10},{10,2},{3,11},{11,3},{4,12},{12,4},... | collective-permute-start | bytes 786440 | tf_op jit(solution)/shard_map/ppermute | solution.py:26
  127.5 3.0 %all-to-all-done.5.query = bf16[4,512,128]{2,1,0:T(8,128)(2,1)S(1)} async-done(((bf16[4,512,128]{2,1,0:T(8,128)(2,1)}), bf16[4,512,128]{2,1,0:T(8,128)(2,1)S(1)}, u32[]{:S(2)}, u32[]{:S(2)}) %all-to-all-start.5) | async-done | bytes 524320 | tf_op jit(solution)/shard_map/all_to_all | solution.py:308
  130.5 6.2 %peers.1 = bf16[4,128,640]{2,1,0:T(8,128)(2,1)} custom-call(s32[45]{0:T(128)S(1)} %pad_add_fusion.1.plan, bf16[4,512,128]{2,1,0:T(8,128)(2,1)S(1)} %all-to-all-done.5.query, bf16[2048,128]{1,0:T(8,128)(2,1)S(1)} %get-tuple-element.18.keys, bf16[2048,256]{1,0:T(8,128)(2,1)S(1)} %get-tuple-element.19.values), custom_call_target="tpu_custom_call" | custom-call | tf_op jit(solution)/shard_map/peers/pallas_call | solution.py:322
  136.7 3.5 %all-to-all-start.6 = ((bf16[4,128,640]{2,1,0:T(8,128)(2,1)}), bf16[4,128,640]{2,1,0:T(8,128)(2,1)S(1)}, u32[]{:S(2)}, u32[]{:S(2)}) async-start(bf16[4,128,640]{2,1,0:T(8,128)(2,1)} %peers.1), calls=%async_computation.6 | async-start | bytes 1310720 | tf_op jit(solution)/shard_map/all_to_all | solution.py:340
  140.2 2.7 %own.1 = bf16[128,640]{1,0:T(8,128)(2,1)S(1)} custom-call(s32[45]{0:T(128)S(1)} %pad_add_fusion.1.plan, bf16[4,512,128]{2,1,0:T(8,128)(2,1)} %query.1, bf16[2048,128]{1,0:T(8,128)(2,1)S(1)} %get-tuple-element.18.keys, bf16[2048,256]{1,0:T(8,128)(2,1)S(1)} %get-tuple-element.19.values), custom_call_target="tpu_custom_call" | custom-call | tf_op jit(solution)/shard_map/own/pallas_call | solution.py:331
  142.8 7.1 %all-to-all-done.6.parts = bf16[4,128,640]{2,1,0:T(8,128)(2,1)S(1)} async-done(((bf16[4,128,640]{2,1,0:T(8,128)(2,1)}), bf16[4,128,640]{2,1,0:T(8,128)(2,1)S(1)}, u32[]{:S(2)}, u32[]{:S(2)}) %all-to-all-start.6) | async-done | bytes 655392 | tf_op jit(solution)/shard_map/all_to_all | solution.py:340
  (64 shorter events, 27.1 us)
Async XLA Ops:
  1.4 33.2 %all-to-all-start = ((bf16[16,8,768]{2,1,0:T(8,128)(2,1)}), bf16[16,8,768]{2,1,0:T(8,128)(2,1)S(1)}, u32[]{:S(2)}, u32[]{:S(2)}) async-start(bf16[16,8,768]{2,1,0:T(8,128)(2,1)} %broadcast_in_dim.86), calls=%async_computation | async-start | bytes 393216 | tf_op jit(solution)/shard_map/all_to_all | solution.py:31
  17.9 10.7 %collective-permute-start = (bf16[128,1024]{1,0:T(8,128)(2,1)S(1)}, bf16[128,1024]{1,0:T(8,128)(2,1)S(1)}, u32[]{:S(2)}, u32[]{:S(2)}) collective-permute-start(bf16[128,1024]{1,0:T(8,128)(2,1)S(1)} %get-tuple-element.25), channel_id=1, source_target_pairs={{0,128},{128,256},{256,384},{384,0},{1,129},{129,257},{257,385},{3... | collective-permute-start | bytes 786440 | tf_op jit(solution)/shard_map/ppermute | solution.py:235
  21.4 18.3 %collective-permute-start.2 = (bf16[128,1024]{1,0:T(8,128)(2,1)S(1)}, bf16[128,1024]{1,0:T(8,128)(2,1)S(1)}, u32[]{:S(2)}, u32[]{:S(2)}) collective-permute-start(bf16[128,1024]{1,0:T(8,128)(2,1)S(1)} %get-tuple-element.23), channel_id=1, source_target_pairs={{0,384},{128,0},{256,128},{384,256},{1,385},{129,1},{257,129},{385... | collective-permute-start | bytes 786440 | tf_op jit(solution)/shard_map/ppermute | solution.py:235
  35.4 11.0 %all-to-all-start.1 = ((bf16[4,16,8,256]{3,2,1,0:T(8,128)(2,1)}), bf16[4,16,8,256]{3,2,1,0:T(8,128)(2,1)S(1)}, u32[]{:S(2)}, u32[]{:S(2)}) async-start(bf16[4,16,8,256]{3,2,1,0:T(8,128)(2,1)} %broadcast_in_dim.87), calls=%async_computation.1 | async-start | bytes 524288 | tf_op jit(solution)/shard_map/all_to_all | solution.py:31
  39.7 7.8 %copy-start.1 = (bf16[128,1024]{1,0:T(8,128)(2,1)}, bf16[128,1024]{1,0:T(8,128)(2,1)S(1)}, u32[]{:S(2)}) copy-start(bf16[128,1024]{1,0:T(8,128)(2,1)S(1)} %collective-permute-done.2.rows3) | copy-start | bytes 786436
  47.4 18.3 %all-to-all-start.2 = ((bf16[4,4,16,8,256]{4,3,2,1,0:T(8,128)(2,1)}), bf16[4,4,16,8,256]{4,3,2,1,0:T(8,128)(2,1)S(1)}, u32[]{:S(2)}, u32[]{:S(2)}) async-start(bf16[4,4,16,8,256]{4,3,2,1,0:T(8,128)(2,1)} %broadcast_in_dim.88), calls=%async_computation.2 | async-start | bytes 2097152 | tf_op jit(solution)/shard_map/all_to_all | solution.py:31
  51.9 13.8 %collective-permute-start.1 = (bf16[128,1024]{1,0:T(8,128)(2,1)S(1)}, bf16[128,1024]{1,0:T(8,128)(2,1)S(1)}, u32[]{:S(2)}, u32[]{:S(2)}) collective-permute-start(bf16[128,1024]{1,0:T(8,128)(2,1)S(1)} %get-tuple-element.24), channel_id=1, source_target_pairs={{0,256},{128,384},{256,0},{384,128},{1,257},{129,385},{257,1},{385... | collective-permute-start | bytes 786440 | tf_op jit(solution)/shard_map/ppermute | solution.py:235
  65.7 3.9 %copy-start.3 = (bf16[128,1024]{1,0:T(8,128)(2,1)}, bf16[128,1024]{1,0:T(8,128)(2,1)S(1)}, u32[]{:S(2)}) copy-start(bf16[128,1024]{1,0:T(8,128)(2,1)S(1)} %collective-permute-done.1.rows2) | copy-start | bytes 786436
  65.7 8.0 %collective-permute-start.3 = (bf16[16,128,256]{2,1,0:T(8,128)(2,1)S(1)}, bf16[16,128,256]{2,1,0:T(8,128)(2,1)}, u32[]{:S(2)}, u32[]{:S(2)}) collective-permute-start(bf16[16,128,256]{2,1,0:T(8,128)(2,1)S(1)} %bitcast.22), channel_id=1, source_target_pairs={{0,8},{8,0},{1,9},{9,1},{2,10},{10,2},{3,11},{11,3},{4,12},{12,4},... | collective-permute-start | bytes 3145736 | tf_op jit(solution)/shard_map/ppermute | solution.py:26
  67.6 0.7 copy-start.5
  68.7 5.0 %copy-start = (bf16[1,128,4096]{2,1,0:T(8,128)(2,1)S(1)}, bf16[1,128,4096]{2,1,0:T(8,128)(2,1)}, u32[]{:S(2)}) copy-start(bf16[1,128,4096]{2,1,0:T(8,128)(2,1)} %param.5) | copy-start | bytes 3145732
  69.6 13.9 %all-to-all-start.3 = ((bf16[4,16,8,512]{3,2,1,0:T(8,128)(2,1)}), bf16[4,16,8,512]{3,2,1,0:T(8,128)(2,1)S(1)}, u32[]{:S(2)}, u32[]{:S(2)}) async-start(bf16[4,16,8,512]{3,2,1,0:T(8,128)(2,1)} %broadcast_in_dim.89), calls=%async_computation.3 | async-start | bytes 1048576 | tf_op jit(solution)/shard_map/all_to_all | solution.py:31
  83.5 9.7 %collective-permute-start.4 = (bf16[4,128,512]{2,1,0:T(8,128)(2,1)S(1)}, bf16[4,128,512]{2,1,0:T(8,128)(2,1)S(1)}, u32[]{:S(2)}, u32[]{:S(2)}) collective-permute-start(bf16[4,128,512]{2,1,0:T(8,128)(2,1)S(1)} %bitcast.24), channel_id=1, source_target_pairs={{0,8},{8,0},{1,9},{9,1},{2,10},{10,2},{3,11},{11,3},{4,12},{12,4},... | collective-permute-start | bytes 1572872 | tf_op jit(solution)/shard_map/ppermute | solution.py:26
  85.6 15.6 %collective-permute-start.5 = (bf16[128,256]{1,0:T(8,128)(2,1)S(1)}, bf16[128,256]{1,0:T(8,128)(2,1)S(1)}, u32[]{:S(2)}, u32[]{:S(2)}) collective-permute-start(bf16[128,256]{1,0:T(8,128)(2,1)S(1)} %key_value.1), channel_id=1, source_target_pairs={{0,64},{16,80},{32,96},{48,112},{64,0},{80,16},{96,32},{112,48},{1... | collective-permute-start | bytes 196616 | tf_op jit(solution)/shard_map/ppermute | solution.py:26
  93.2 1.0 copy-start.2
  94.1 0.9 copy-start.4
  97.5 19.2 %all-to-all-start.4 = ((f32[4,128,512]{2,1,0:T(8,128)}), f32[4,128,512]{2,1,0:T(8,128)S(1)}, u32[]{:S(2)}, u32[]{:S(2)}) async-start(f32[4,128,512]{2,1,0:T(8,128)} %project.1), calls=%async_computation.4 | async-start | bytes 2097152 | tf_op jit(solution)/shard_map/all_to_all | solution.py:291
  101.2 8.4 %collective-permute-start.6 = (bf16[256,256]{1,0:T(8,128)(2,1)S(1)}, bf16[256,256]{1,0:T(8,128)(2,1)S(1)}, u32[]{:S(2)}, u32[]{:S(2)}) collective-permute-start(bf16[256,256]{1,0:T(8,128)(2,1)S(1)} %pad_maximum_fusion.1), channel_id=1, source_target_pairs={{0,32},{16,48},{32,0},{48,16},{64,96},{80,112},{96,64},{112,80},{1... | collective-permute-start | bytes 393224 | tf_op jit(solution)/shard_map/ppermute | solution.py:26
  109.6 13.5 %collective-permute-start.7 = (bf16[512,256]{1,0:T(8,128)(2,1)S(1)}, bf16[512,256]{1,0:T(8,128)(2,1)S(1)}, u32[]{:S(2)}, u32[]{:S(2)}) collective-permute-start(bf16[512,256]{1,0:T(8,128)(2,1)S(1)} %pad_maximum_fusion.own_near), channel_id=1, source_target_pairs={{0,16},{16,0},{32,48},{48,32},{64,80},{80,64},{96,112},{112,96},{1... | collective-permute-start | bytes 786440 | tf_op jit(solution)/shard_map/ppermute | solution.py:26
  117.7 12.8 %all-to-all-start.5 = ((bf16[4,512,128]{2,1,0:T(8,128)(2,1)}), bf16[4,512,128]{2,1,0:T(8,128)(2,1)S(1)}, u32[]{:S(2)}, u32[]{:S(2)}) async-start(bf16[4,512,128]{2,1,0:T(8,128)(2,1)} %query.1), calls=%async_computation.5 | async-start | bytes 1048576 | tf_op jit(solution)/shard_map/all_to_all | solution.py:308
  121.2 4.8 %collective-permute-start.8 = (bf16[512,256]{1,0:T(8,128)(2,1)S(1)}, bf16[512,256]{1,0:T(8,128)(2,1)S(1)}, u32[]{:S(2)}, u32[]{:S(2)}) collective-permute-start(bf16[512,256]{1,0:T(8,128)(2,1)S(1)} %pad_maximum_fusion.own_near), channel_id=1, source_target_pairs={{0,8},{8,0},{1,9},{9,1},{2,10},{10,2},{3,11},{11,3},{4,12},{12,4},... | collective-permute-start | bytes 786440 | tf_op jit(solution)/shard_map/ppermute | solution.py:26
  123.1 3.6 %collective-permute-start.9 = (bf16[512,256]{1,0:T(8,128)(2,1)S(1)}, bf16[512,256]{1,0:T(8,128)(2,1)S(1)}, u32[]{:S(2)}, u32[]{:S(2)}) collective-permute-start(bf16[512,256]{1,0:T(8,128)(2,1)S(1)} %collective-permute-done.7.own_far), channel_id=1, source_target_pairs={{0,8},{8,0},{1,9},{9,1},{2,10},{10,2},{3,11},{11,3},{4,12},{12,4},... | collective-permute-start | bytes 786440 | tf_op jit(solution)/shard_map/ppermute | solution.py:26
  136.7 13.2 %all-to-all-start.6 = ((bf16[4,128,640]{2,1,0:T(8,128)(2,1)}), bf16[4,128,640]{2,1,0:T(8,128)(2,1)S(1)}, u32[]{:S(2)}, u32[]{:S(2)}) async-start(bf16[4,128,640]{2,1,0:T(8,128)(2,1)} %peers.1), calls=%async_computation.6 | async-start | bytes 1310720 | tf_op jit(solution)/shard_map/all_to_all | solution.py:340

commit v4 on v3

--- a/solution.py
+++ b/solution.py
@@ -234,14 +234,11 @@
         if shift:
             piece = lax.ppermute(piece, "y", [(i, (i + shift) % 4) for i in range(4)])
         sliced.append(piece)
-    along_z = after(along_z, sliced[1])
-    narrow = spread(along_z[:, :, : 2 * HEAD], "x", 4)
-    narrow = after(narrow, sliced[3])
-    narrow = spread(narrow, "y", 4).reshape(16, ROWS, 2 * HEAD)
-    narrow = after(narrow, sliced[2])
-    narrow_across = swap(narrow, "core", 2, 1)
-    wide, _ = lax.optimization_barrier((along_z[:, :, 2 * HEAD :], narrow))
-    wide = spread(wide, "x", 4).reshape(4, ROWS, HEADS * HEAD)
+    along_z = after(along_z, sliced[1], sliced[2])
+    along_x = after(spread(along_z, "x", 4), sliced[3]).reshape(4, ROWS, 768)
+    wide = along_x[:, :, 2 * HEAD :]
+    wide_across = swap(wide, "core", 2, 1)
+    narrow = spread(along_x[:, :, : 2 * HEAD], "y", 4).reshape(16, ROWS, 2 * HEAD)
 
     table = stretch_table.reshape(4, 8, 2, 2)
     own_stretches = table[y, zl, core]
@@ -268,6 +265,18 @@
     where = jnp.stack([y, core]).astype(jnp.int32)
     flip = (own_stretches[:1] > own_stretches[1:]).astype(jnp.int32)
 
+    query_part = pl.pallas_call(
+        project_kernel,
+        out_shape=pltpu.VMEM((4, ROWS, HEADS * HEAD), f32),
+        in_specs=[smem] + [vmem] * 6,
+        out_specs=vmem,
+        scratch_shapes=[pltpu.VMEM((1024, HEADS * HEAD), bf16)],
+        compiler_params=limits,
+        name="project",
+    )(where, *in_vmem(*sliced, wide, wide_across))
+    narrow, query_part = lax.optimization_barrier((narrow, query_part))
+    narrow_across = swap(narrow, "core", 2, 1)
+    query_part = lax.all_to_all(query_part, "y", 0, 0)
     key_value = pl.pallas_call(
         key_value_kernel,
         out_shape=pltpu.VMEM((ROWS, 2 * HEAD), bf16),
@@ -277,18 +286,6 @@
         compiler_params=limits,
         name="key_value",
     )(where, *in_vmem(rows, narrow, narrow_across, cosine, sine))
-    wide = after(wide, key_value)
-    wide_across = swap(wide, "core", 2, 1)
-    query_part = pl.pallas_call(
-        project_kernel,
-        out_shape=pltpu.VMEM((4, ROWS, HEADS * HEAD), f32),
-        in_specs=[smem] + [vmem] * 6,
-        out_specs=vmem,
-        scratch_shapes=[pltpu.VMEM((1024, HEADS * HEAD), bf16)],
-        compiler_params=limits,
-        name="project",
-    )(where, *in_vmem(*sliced, wide, wide_across))
-    query_part = lax.all_to_all(query_part, "y", 0, 0)
 
     step = swap(key_value, "zl", 8, 4)
     step = jnp.concatenate([key_value, step], axis=0)
@@ -304,7 +301,7 @@
         out_specs=vmem,
         compiler_params=limits,
         name="query",
-    )(flip, *in_vmem(query_part, cosine, sine))
+    )(flip, *in_vmem(after(query_part, key_value), cosine, sine))
     queries = lax.all_to_all(query, "y", 0, 0)
 
     keys, values = pl.pallas_call(

time: 153 us -> 147 us (0.961)
  waiting for transfers between devices: 52.1 us -> 44.5 us
  starting transfers between devices: 70.3 us -> 73.6 us
    all_to_all x4 -> x3, waiting for transfers between devices: 20.5 us -> 9.17 us  [spread(): return lax.all_to_all(copies, axis, 0, 0)]
    ppermute x7, starting transfers between devices: 19.9 us -> 25.9 us  [swap(): return lax.ppermute(value, axis, [(i, i ^ distance) for i in range(size)])]
    ppermute x7, waiting for transfers between devices: 6.86 us -> 11.3 us  [swap(): return lax.ppermute(value, axis, [(i, i ^ distance) for i in range(size)])]
    all_to_all x4 -> x3, starting transfers between devices: 27.4 us -> 24.6 us  [spread(): return lax.all_to_all(copies, axis, 0, 0)]
    all_to_all x1, waiting for transfers between devices: 2.8 us -> 0.01 us  [on_device(): query_part = lax.all_to_all(query_part, 'y', 0, 0)]
    unnamed x12 -> x6, local copies, waits for them, and re-layouts: 2.58 us -> 0.7 us
    broadcast_in_dim x4 -> x3, local copies, waits for them, and re-layouts: 3.37 us -> 2.83 us  [spread(): copies = jnp.broadcast_to(value[None], (size,) + value.shape)]
  transfers between devices with their start and end apart: 17 -> 16, of which waited for: 10 -> 11; matrix products, arithmetic and copies ran while one was open for 4% -> 4% of each run, Pallas kernels for 6% -> 6%
where the time goes in v4:
time: 147 us; the launch traced here: 146 us
  starting transfers between devices  73.6 us (50%)
  waiting for transfers between devices  44.5 us (30%)
  Pallas kernels  16.8 us (11%)
  local copies, waits for them, and re-layouts  7.04 us (5%)
  other arithmetic  2.41 us (2%)
  between operations  1.54 us (1%)
    ppermute x7, starting transfers between devices, swap(): return lax.ppermute(value, axis, [(i, i ^ distance) for i in range(size)])  25.9 us
    all_to_all x3, starting transfers between devices, spread(): return lax.all_to_all(copies, axis, 0, 0)  24.6 us
    ppermute x3, waiting for transfers between devices, on_device(): piece = lax.ppermute(piece, 'y', [(i, (i + shift) % 4) for i in range(4)])  13.2 us
    ppermute x3, starting transfers between devices, on_device(): piece = lax.ppermute(piece, 'y', [(i, (i + shift) % 4) for i in range(4)])  12.5 us
    ppermute x7, waiting for transfers between devices, swap(): return lax.ppermute(value, axis, [(i, i ^ distance) for i in range(size)])  11.3 us
    all_to_all x3, waiting for transfers between devices, spread(): return lax.all_to_all(copies, axis, 0, 0)  9.17 us
    all_to_all x1, waiting for transfers between devices, on_device(): partial = lax.all_to_all(partial, 'y', 0, 0)  7.53 us
    pallas_call x1, Pallas kernels, on_device(): pl.pallas_call(peers_kernel, out_shape=pltpu.VMEM((4, ROWS, HEADS * HEAD...  6.07 us
  transfers between devices with their start and end apart: 16, of which 11 were waited for; matrix products, arithmetic and copies ran while one was open for 4% of the time, Pallas kernels for 6%

profile of v4, /device:TPU:32, one launch (start us, length us, event | category | flops | bytes accessed | tf_op | source)
XLA Modules:
  0.0 145.9 jit_solution(1261419730316380379)
XLA Ops:
  1.4 15.2 %all-to-all-start = ((bf16[16,8,768]{2,1,0:T(8,128)(2,1)}), bf16[16,8,768]{2,1,0:T(8,128)(2,1)S(1)}, u32[]{:S(2)}, u32[]{:S(2)}) async-start(bf16[16,8,768]{2,1,0:T(8,128)(2,1)} %broadcast_in_dim.80), calls=%async_computation | async-start | bytes 393216 | tf_op jit(solution)/shard_map/all_to_all | solution.py:31
  17.9 5.1 %collective-permute-start.1 = (bf16[128,1024]{1,0:T(8,128)(2,1)S(1)}, bf16[128,1024]{1,0:T(8,128)(2,1)S(1)}, u32[]{:S(2)}, u32[]{:S(2)}) collective-permute-start(bf16[128,1024]{1,0:T(8,128)(2,1)S(1)} %get-tuple-element.25), channel_id=1, source_target_pairs={{0,256},{128,384},{256,0},{384,128},{1,257},{129,385},{257,1},{385... | collective-permute-start | bytes 786440 | tf_op jit(solution)/shard_map/ppermute | solution.py:235
  23.0 2.6 %collective-permute-start = (bf16[128,1024]{1,0:T(8,128)(2,1)S(1)}, bf16[128,1024]{1,0:T(8,128)(2,1)S(1)}, u32[]{:S(2)}, u32[]{:S(2)}) collective-permute-start(bf16[128,1024]{1,0:T(8,128)(2,1)S(1)} %get-tuple-element.26), channel_id=1, source_target_pairs={{0,128},{128,256},{256,384},{384,0},{1,129},{129,257},{257,385},{3... | collective-permute-start | bytes 786440 | tf_op jit(solution)/shard_map/ppermute | solution.py:235
  25.6 4.9 %collective-permute-done.1.rows2 = bf16[128,1024]{1,0:T(8,128)(2,1)S(1)} collective-permute-done((bf16[128,1024]{1,0:T(8,128)(2,1)S(1)}, bf16[128,1024]{1,0:T(8,128)(2,1)S(1)}, u32[]{:S(2)}, u32[]{:S(2)}) %collective-permute-start.1) | collective-permute-done | bytes 262176 | tf_op jit(solution)/shard_map/ppermute | solution.py:235
  30.5 4.2 %collective-permute-done.rows1 = bf16[128,1024]{1,0:T(8,128)(2,1)S(1)} collective-permute-done((bf16[128,1024]{1,0:T(8,128)(2,1)S(1)}, bf16[128,1024]{1,0:T(8,128)(2,1)S(1)}, u32[]{:S(2)}, u32[]{:S(2)}) %collective-permute-start) | collective-permute-done | bytes 262176 | tf_op jit(solution)/shard_map/ppermute | solution.py:235
  35.7 4.3 %all-to-all-start.1 = ((bf16[4,16,8,768]{3,2,1,0:T(8,128)(2,1)}), bf16[4,16,8,768]{3,2,1,0:T(8,128)(2,1)S(1)}, u32[]{:S(2)}, u32[]{:S(2)}) async-start(bf16[4,16,8,768]{3,2,1,0:T(8,128)(2,1)} %broadcast_in_dim.81), calls=%async_computation.1 | async-start | bytes 1572864 | tf_op jit(solution)/shard_map/all_to_all | solution.py:31
  39.9 4.8 %collective-permute-start.2 = (bf16[128,1024]{1,0:T(8,128)(2,1)S(1)}, bf16[128,1024]{1,0:T(8,128)(2,1)S(1)}, u32[]{:S(2)}, u32[]{:S(2)}) collective-permute-start(bf16[128,1024]{1,0:T(8,128)(2,1)S(1)} %get-tuple-element.24), channel_id=1, source_target_pairs={{0,384},{128,0},{256,128},{384,256},{1,385},{129,1},{257,129},{385... | collective-permute-start | bytes 786440 | tf_op jit(solution)/shard_map/ppermute | solution.py:235
  44.8 4.0 %collective-permute-done.2.rows3 = bf16[128,1024]{1,0:T(8,128)(2,1)S(1)} collective-permute-done((bf16[128,1024]{1,0:T(8,128)(2,1)S(1)}, bf16[128,1024]{1,0:T(8,128)(2,1)S(1)}, u32[]{:S(2)}, u32[]{:S(2)}) %collective-permute-start.2) | collective-permute-done | bytes 262176 | tf_op jit(solution)/shard_map/ppermute | solution.py:235
  48.8 2.6 %all-to-all-done.1 = bf16[4,16,8,768]{3,2,1,0:T(8,128)(2,1)S(1)} async-done(((bf16[4,16,8,768]{3,2,1,0:T(8,128)(2,1)}), bf16[4,16,8,768]{3,2,1,0:T(8,128)(2,1)S(1)}, u32[]{:S(2)}, u32[]{:S(2)}) %all-to-all-start.1) | async-done | bytes 786464 | tf_op jit(solution)/shard_map/all_to_all | solution.py:31
  52.7 5.1 %all-to-all-start.2 = ((bf16[4,4,128,256]{3,2,1,0:T(8,128)(2,1)}), bf16[4,4,128,256]{3,2,1,0:T(8,128)(2,1)S(1)}, u32[]{:S(2)}, u32[]{:S(2)}) async-start(bf16[4,4,128,256]{3,2,1,0:T(8,128)(2,1)} %broadcast_in_dim.82), calls=%async_computation.2 | async-start | bytes 2097152 | tf_op jit(solution)/shard_map/all_to_all | solution.py:31
  65.1 6.5 %all-to-all-done.2 = bf16[4,4,128,256]{3,2,1,0:T(8,128)(2,1)S(1)} async-done(((bf16[4,4,128,256]{3,2,1,0:T(8,128)(2,1)}), bf16[4,4,128,256]{3,2,1,0:T(8,128)(2,1)S(1)}, u32[]{:S(2)}, u32[]{:S(2)}) %all-to-all-start.2) | async-done | bytes 1048608 | tf_op jit(solution)/shard_map/all_to_all | solution.py:31
  74.2 3.6 %all-to-all-start.3 = ((f32[4,128,512]{2,1,0:T(8,128)}), f32[4,128,512]{2,1,0:T(8,128)S(1)}, u32[]{:S(2)}, u32[]{:S(2)}) async-start(f32[4,128,512]{2,1,0:T(8,128)} %project.1), calls=%async_computation.3 | async-start | bytes 2097152 | tf_op jit(solution)/shard_map/all_to_all | solution.py:279
  79.9 7.6 %collective-permute-start.5 = (bf16[128,256]{1,0:T(8,128)(2,1)S(1)}, bf16[128,256]{1,0:T(8,128)(2,1)S(1)}, u32[]{:S(2)}, u32[]{:S(2)}) collective-permute-start(bf16[128,256]{1,0:T(8,128)(2,1)S(1)} %key_value.1), channel_id=1, source_target_pairs={{0,64},{16,80},{32,96},{48,112},{64,0},{80,16},{96,32},{112,48},{1... | collective-permute-start | bytes 196616 | tf_op jit(solution)/shard_map/ppermute | solution.py:26
  87.7 5.5 %collective-permute-done.5 = bf16[128,256]{1,0:T(8,128)(2,1)S(1)} collective-permute-done((bf16[128,256]{1,0:T(8,128)(2,1)S(1)}, bf16[128,256]{1,0:T(8,128)(2,1)S(1)}, u32[]{:S(2)}, u32[]{:S(2)}) %collective-permute-start.5) | collective-permute-done | bytes 65568 | tf_op jit(solution)/shard_map/ppermute | solution.py:26
  93.2 4.8 %collective-permute-start.6 = (bf16[256,256]{1,0:T(8,128)(2,1)S(1)}, bf16[256,256]{1,0:T(8,128)(2,1)S(1)}, u32[]{:S(2)}, u32[]{:S(2)}) collective-permute-start(bf16[256,256]{1,0:T(8,128)(2,1)S(1)} %pad_maximum_fusion.1), channel_id=1, source_target_pairs={{0,32},{16,48},{32,0},{48,16},{64,96},{80,112},{96,64},{112,80},{1... | collective-permute-start | bytes 393224 | tf_op jit(solution)/shard_map/ppermute | solution.py:26
  98.1 4.4 %collective-permute-done.6 = bf16[256,256]{1,0:T(8,128)(2,1)S(1)} collective-permute-done((bf16[256,256]{1,0:T(8,128)(2,1)S(1)}, bf16[256,256]{1,0:T(8,128)(2,1)S(1)}, u32[]{:S(2)}, u32[]{:S(2)}) %collective-permute-start.6) | collective-permute-done | bytes 131104 | tf_op jit(solution)/shard_map/ppermute | solution.py:26
  102.5 5.3 %collective-permute-start.7 = (bf16[512,256]{1,0:T(8,128)(2,1)S(1)}, bf16[512,256]{1,0:T(8,128)(2,1)S(1)}, u32[]{:S(2)}, u32[]{:S(2)}) collective-permute-start(bf16[512,256]{1,0:T(8,128)(2,1)S(1)} %pad_maximum_fusion.own_near), channel_id=1, source_target_pairs={{0,16},{16,0},{32,48},{48,32},{64,80},{80,64},{96,112},{112,96},{1... | collective-permute-start | bytes 786440 | tf_op jit(solution)/shard_map/ppermute | solution.py:26
  111.2 3.5 %all-to-all-start.4 = ((bf16[4,512,128]{2,1,0:T(8,128)(2,1)}), bf16[4,512,128]{2,1,0:T(8,128)(2,1)S(1)}, u32[]{:S(2)}, u32[]{:S(2)}) async-start(bf16[4,512,128]{2,1,0:T(8,128)(2,1)} %query.1), calls=%async_computation.4 | async-start | bytes 1048576 | tf_op jit(solution)/shard_map/all_to_all | solution.py:305
  116.6 2.4 %collective-permute-start.9 = (bf16[512,256]{1,0:T(8,128)(2,1)S(1)}, bf16[512,256]{1,0:T(8,128)(2,1)S(1)}, u32[]{:S(2)}, u32[]{:S(2)}) collective-permute-start(bf16[512,256]{1,0:T(8,128)(2,1)S(1)} %collective-permute-done.7.own_far), channel_id=1, source_target_pairs={{0,8},{8,0},{1,9},{9,1},{2,10},{10,2},{3,11},{11,3},{4,12},{12,4},... | collective-permute-start | bytes 786440 | tf_op jit(solution)/shard_map/ppermute | solution.py:26
  121.0 3.3 %all-to-all-done.4.query = bf16[4,512,128]{2,1,0:T(8,128)(2,1)S(1)} async-done(((bf16[4,512,128]{2,1,0:T(8,128)(2,1)}), bf16[4,512,128]{2,1,0:T(8,128)(2,1)S(1)}, u32[]{:S(2)}, u32[]{:S(2)}) %all-to-all-start.4) | async-done | bytes 524320 | tf_op jit(solution)/shard_map/all_to_all | solution.py:305
  124.3 6.1 %peers.1 = bf16[4,128,640]{2,1,0:T(8,128)(2,1)} custom-call(s32[45]{0:T(128)S(1)} %pad_add_fusion.1.plan, bf16[4,512,128]{2,1,0:T(8,128)(2,1)S(1)} %all-to-all-done.4.query, bf16[2048,128]{1,0:T(8,128)(2,1)S(1)} %get-tuple-element.18.keys, bf16[2048,256]{1,0:T(8,128)(2,1)S(1)} %get-tuple-element.19.values), custom_call_target="tpu_custom_call" | custom-call | tf_op jit(solution)/shard_map/peers/pallas_call | solution.py:319
  130.3 3.5 %all-to-all-start.5 = ((bf16[4,128,640]{2,1,0:T(8,128)(2,1)}), bf16[4,128,640]{2,1,0:T(8,128)(2,1)S(1)}, u32[]{:S(2)}, u32[]{:S(2)}) async-start(bf16[4,128,640]{2,1,0:T(8,128)(2,1)} %peers.1), calls=%async_computation.5 | async-start | bytes 1310720 | tf_op jit(solution)/shard_map/all_to_all | solution.py:337
  133.8 2.6 %own.1 = bf16[128,640]{1,0:T(8,128)(2,1)S(1)} custom-call(s32[45]{0:T(128)S(1)} %pad_add_fusion.1.plan, bf16[4,512,128]{2,1,0:T(8,128)(2,1)} %query.1, bf16[2048,128]{1,0:T(8,128)(2,1)S(1)} %get-tuple-element.18.keys, bf16[2048,256]{1,0:T(8,128)(2,1)S(1)} %get-tuple-element.19.values), custom_call_target="tpu_custom_call" | custom-call | tf_op jit(solution)/shard_map/own/pallas_call | solution.py:328
  136.4 7.5 %all-to-all-done.5.parts = bf16[4,128,640]{2,1,0:T(8,128)(2,1)S(1)} async-done(((bf16[4,128,640]{2,1,0:T(8,128)(2,1)}), bf16[4,128,640]{2,1,0:T(8,128)(2,1)S(1)}, u32[]{:S(2)}, u32[]{:S(2)}) %all-to-all-start.5) | async-done | bytes 655392 | tf_op jit(solution)/shard_map/all_to_all | solution.py:337
  (55 shorter events, 24.7 us)
Async XLA Ops:
  1.4 33.3 %all-to-all-start = ((bf16[16,8,768]{2,1,0:T(8,128)(2,1)}), bf16[16,8,768]{2,1,0:T(8,128)(2,1)S(1)}, u32[]{:S(2)}, u32[]{:S(2)}) async-start(bf16[16,8,768]{2,1,0:T(8,128)(2,1)} %broadcast_in_dim.80), calls=%async_computation | async-start | bytes 393216 | tf_op jit(solution)/shard_map/all_to_all | solution.py:31
  17.9 12.6 %collective-permute-start.1 = (bf16[128,1024]{1,0:T(8,128)(2,1)S(1)}, bf16[128,1024]{1,0:T(8,128)(2,1)S(1)}, u32[]{:S(2)}, u32[]{:S(2)}) collective-permute-start(bf16[128,1024]{1,0:T(8,128)(2,1)S(1)} %get-tuple-element.25), channel_id=1, source_target_pairs={{0,256},{128,384},{256,0},{384,128},{1,257},{129,385},{257,1},{385... | collective-permute-start | bytes 786440 | tf_op jit(solution)/shard_map/ppermute | solution.py:235
  23.0 11.7 %collective-permute-start = (bf16[128,1024]{1,0:T(8,128)(2,1)S(1)}, bf16[128,1024]{1,0:T(8,128)(2,1)S(1)}, u32[]{:S(2)}, u32[]{:S(2)}) collective-permute-start(bf16[128,1024]{1,0:T(8,128)(2,1)S(1)} %get-tuple-element.26), channel_id=1, source_target_pairs={{0,128},{128,256},{256,384},{384,0},{1,129},{129,257},{257,385},{3... | collective-permute-start | bytes 786440 | tf_op jit(solution)/shard_map/ppermute | solution.py:235
  35.7 15.8 %all-to-all-start.1 = ((bf16[4,16,8,768]{3,2,1,0:T(8,128)(2,1)}), bf16[4,16,8,768]{3,2,1,0:T(8,128)(2,1)S(1)}, u32[]{:S(2)}, u32[]{:S(2)}) async-start(bf16[4,16,8,768]{3,2,1,0:T(8,128)(2,1)} %broadcast_in_dim.81), calls=%async_computation.1 | async-start | bytes 1572864 | tf_op jit(solution)/shard_map/all_to_all | solution.py:31
  39.9 8.9 %collective-permute-start.2 = (bf16[128,1024]{1,0:T(8,128)(2,1)S(1)}, bf16[128,1024]{1,0:T(8,128)(2,1)S(1)}, u32[]{:S(2)}, u32[]{:S(2)}) collective-permute-start(bf16[128,1024]{1,0:T(8,128)(2,1)S(1)} %get-tuple-element.24), channel_id=1, source_target_pairs={{0,384},{128,0},{256,128},{384,256},{1,385},{129,1},{257,129},{385... | collective-permute-start | bytes 786440 | tf_op jit(solution)/shard_map/ppermute | solution.py:235
  51.5 1.3 copy-start.1
  52.7 18.9 %all-to-all-start.2 = ((bf16[4,4,128,256]{3,2,1,0:T(8,128)(2,1)}), bf16[4,4,128,256]{3,2,1,0:T(8,128)(2,1)S(1)}, u32[]{:S(2)}, u32[]{:S(2)}) async-start(bf16[4,4,128,256]{3,2,1,0:T(8,128)(2,1)} %broadcast_in_dim.82), calls=%async_computation.2 | async-start | bytes 2097152 | tf_op jit(solution)/shard_map/all_to_all | solution.py:31
  58.9 3.8 %collective-permute-start.3 = (bf16[4,128,512]{2,1,0:T(8,128)(2,1)S(1)}, bf16[4,128,512]{2,1,0:T(8,128)(2,1)S(1)}, u32[]{:S(2)}, u32[]{:S(2)}) collective-permute-start(bf16[4,128,512]{2,1,0:T(8,128)(2,1)S(1)} %slice.27.mine), channel_id=1, source_target_pairs={{0,8},{8,0},{1,9},{9,1},{2,10},{10,2},{3,11},{11,3},{4,12},{12,4},... | collective-permute-start | bytes 1572872 | tf_op jit(solution)/shard_map/ppermute | solution.py:26
  60.8 0.7 copy-start.2
  71.6 6.3 %collective-permute-start.4 = (bf16[16,128,256]{2,1,0:T(8,128)(2,1)S(1)}, bf16[16,128,256]{2,1,0:T(8,128)(2,1)}, u32[]{:S(2)}, u32[]{:S(2)}) collective-permute-start(bf16[16,128,256]{2,1,0:T(8,128)(2,1)S(1)} %bitcast.22), channel_id=1, source_target_pairs={{0,8},{8,0},{1,9},{9,1},{2,10},{10,2},{3,11},{11,3},{4,12},{12,4},... | collective-permute-start | bytes 3145736 | tf_op jit(solution)/shard_map/ppermute | solution.py:26
  74.2 3.7 %copy-start = (bf16[1,128,4096]{2,1,0:T(8,128)(2,1)S(1)}, bf16[1,128,4096]{2,1,0:T(8,128)(2,1)}, u32[]{:S(2)}) copy-start(bf16[1,128,4096]{2,1,0:T(8,128)(2,1)} %param.5) | copy-start | bytes 3145732
  74.2 36.0 %all-to-all-start.3 = ((f32[4,128,512]{2,1,0:T(8,128)}), f32[4,128,512]{2,1,0:T(8,128)S(1)}, u32[]{:S(2)}, u32[]{:S(2)}) async-start(f32[4,128,512]{2,1,0:T(8,128)} %project.1), calls=%async_computation.3 | async-start | bytes 2097152 | tf_op jit(solution)/shard_map/all_to_all | solution.py:279
  79.9 13.2 %collective-permute-start.5 = (bf16[128,256]{1,0:T(8,128)(2,1)S(1)}, bf16[128,256]{1,0:T(8,128)(2,1)S(1)}, u32[]{:S(2)}, u32[]{:S(2)}) collective-permute-start(bf16[128,256]{1,0:T(8,128)(2,1)S(1)} %key_value.1), channel_id=1, source_target_pairs={{0,64},{16,80},{32,96},{48,112},{64,0},{80,16},{96,32},{112,48},{1... | collective-permute-start | bytes 196616 | tf_op jit(solution)/shard_map/ppermute | solution.py:26
  93.2 9.2 %collective-permute-start.6 = (bf16[256,256]{1,0:T(8,128)(2,1)S(1)}, bf16[256,256]{1,0:T(8,128)(2,1)S(1)}, u32[]{:S(2)}, u32[]{:S(2)}) collective-permute-start(bf16[256,256]{1,0:T(8,128)(2,1)S(1)} %pad_maximum_fusion.1), channel_id=1, source_target_pairs={{0,32},{16,48},{32,0},{48,16},{64,96},{80,112},{96,64},{112,80},{1... | collective-permute-start | bytes 393224 | tf_op jit(solution)/shard_map/ppermute | solution.py:26
  102.5 14.1 %collective-permute-start.7 = (bf16[512,256]{1,0:T(8,128)(2,1)S(1)}, bf16[512,256]{1,0:T(8,128)(2,1)S(1)}, u32[]{:S(2)}, u32[]{:S(2)}) collective-permute-start(bf16[512,256]{1,0:T(8,128)(2,1)S(1)} %pad_maximum_fusion.own_near), channel_id=1, source_target_pairs={{0,16},{16,0},{32,48},{48,32},{64,80},{80,64},{96,112},{112,96},{1... | collective-permute-start | bytes 786440 | tf_op jit(solution)/shard_map/ppermute | solution.py:26
  111.2 13.1 %all-to-all-start.4 = ((bf16[4,512,128]{2,1,0:T(8,128)(2,1)}), bf16[4,512,128]{2,1,0:T(8,128)(2,1)S(1)}, u32[]{:S(2)}, u32[]{:S(2)}) async-start(bf16[4,512,128]{2,1,0:T(8,128)(2,1)} %query.1), calls=%async_computation.4 | async-start | bytes 1048576 | tf_op jit(solution)/shard_map/all_to_all | solution.py:305
  114.7 4.8 %collective-permute-start.8 = (bf16[512,256]{1,0:T(8,128)(2,1)S(1)}, bf16[512,256]{1,0:T(8,128)(2,1)S(1)}, u32[]{:S(2)}, u32[]{:S(2)}) collective-permute-start(bf16[512,256]{1,0:T(8,128)(2,1)S(1)} %pad_maximum_fusion.own_near), channel_id=1, source_target_pairs={{0,8},{8,0},{1,9},{9,1},{2,10},{10,2},{3,11},{11,3},{4,12},{12,4},... | collective-permute-start | bytes 786440 | tf_op jit(solution)/shard_map/ppermute | solution.py:26
  116.6 3.6 %collective-permute-start.9 = (bf16[512,256]{1,0:T(8,128)(2,1)S(1)}, bf16[512,256]{1,0:T(8,128)(2,1)S(1)}, u32[]{:S(2)}, u32[]{:S(2)}) collective-permute-start(bf16[512,256]{1,0:T(8,128)(2,1)S(1)} %collective-permute-done.7.own_far), channel_id=1, source_target_pairs={{0,8},{8,0},{1,9},{9,1},{2,10},{10,2},{3,11},{11,3},{4,12},{12,4},... | collective-permute-start | bytes 786440 | tf_op jit(solution)/shard_map/ppermute | solution.py:26
  130.3 13.6 %all-to-all-start.5 = ((bf16[4,128,640]{2,1,0:T(8,128)(2,1)}), bf16[4,128,640]{2,1,0:T(8,128)(2,1)S(1)}, u32[]{:S(2)}, u32[]{:S(2)}) async-start(bf16[4,128,640]{2,1,0:T(8,128)(2,1)} %peers.1), calls=%async_computation.5 | async-start | bytes 1310720 | tf_op jit(solution)/shard_map/all_to_all | solution.py:337
